TPU v7x, 256 devices: a whole 4x4x8 slice. The times are simulated.
256 devices in a mesh: cfg: 2 (over core), seq: 32 (over y, z), blk: 4 (over x).
Axes of the slice: x: 4, y: 4, z: 8, core: 2. Of those that a mesh axis runs over, the one named last changes fastest.
Arguments:
- queries: bfloat16 [2, 12288, 1536], P('cfg', 'seq', 'blk'), may hold values from -20 to 20
- keys: bfloat16 [2, 12288, 1536], P('cfg', 'seq', 'blk'), may hold values from -20 to 20
- values: bfloat16 [2, 12288, 1536], P('cfg', 'seq', 'blk'), may hold values from -6 to 6
- residual: bfloat16 [2, 12288, 1536], P('cfg', 'seq'), may hold values from -6 to 6
- w_out: bfloat16 [1536, 1536], P('blk'), may hold values from -0.15625 to 0.15625
- w_up: bfloat16 [1536, 6144], P(None, 'blk'), may hold values from -0.15625 to 0.15625
- w_down: bfloat16 [6144, 1536], P('blk'), may hold values from -0.078125 to 0.078125
- modulation: float32 [3, 4, 1536], replicated, may hold values from -3 to 3
- guide_scale: float32 [3], replicated, may hold values from 1.5 to 4
- slot_clip: int32 [12288], P('seq'), may hold values from 0 to 3, as said below
- owner: int32 [12288, 1], P('seq'), may hold values from 0 to 31; in each aligned block of 192 rows (0 to 191, 192 to 383, ...) at most 12 rows name the same one
Outputs:
- returned: bfloat16 [2, 12288, 1536], P('cfg', 'seq', 'blk')
Inputs may be any that keep to these rules, and one draw needn't show every extreme that they name: `slot_clip`: each device's block of 384 slots holds its live slots first and its padding slots, marked 3, last; live slots, counted block after block, are dealt to the clips in turn (the t-th live slot belongs to clip t mod 3), so each clip has 3584 live slots. In each aligned half-block of 192 slots no owner is named more than 12 times.
All inputs are finite; a program needn't handle non-finite values.
Results may differ from a plain program's by a relative error of at most 0.017.
Values may be sent and summed in bfloat16 or wider, within the bound.
A program may use at most 128 MiB of HBM per device.

v0:
```python
import math

import jax
import jax.numpy as jnp
from jax import lax
from jax.sharding import PartitionSpec as P

D = 1536
HEAD_DIM = 128
CLIPS = 3


NEG_FILL = -1e30


def swapped(value, axis, bit):
    mask = 2**bit
    pairs = [(source, source ^ mask) for source in range(lax.axis_size(axis))]
    return lax.ppermute(value, axis, pairs)


def shards(
    queries, keys, values, residual, w_out, w_up, w_down, modulation, guide_scale, slot_clip, owner
):
    query_here = queries[0]
    slots, width = query_here.shape
    heads_here = width // HEAD_DIM
    factor = 1.0 / math.sqrt(HEAD_DIM)
    live = slot_clip < CLIPS
    query_heads = query_here.reshape(slots, heads_here, HEAD_DIM)

    def absorb_block(carry, key_block, value_block, clip_block):
        count = key_block.shape[0]
        kept = (clip_block[None, :] == slot_clip[:, None]) & live[:, None]
        best, total, accum = carry
        key_heads = key_block.reshape(count, heads_here, HEAD_DIM)
        value_heads = value_block.reshape(count, heads_here, HEAD_DIM)
        scores = (
            jnp.einsum("qhd,khd->hqk", query_heads, key_heads, preferred_element_type=jnp.float32)
            * factor
        )
        scores = jnp.where(kept[None], scores, NEG_FILL)
        new_best = jnp.maximum(best, jnp.max(scores, axis=-1))
        fade = jnp.exp(best - new_best)
        probs = jnp.exp(scores - new_best[..., None])
        total = total * fade + jnp.sum(probs, axis=-1)
        added = jnp.einsum(
            "hqk,khd->qhd",
            probs.astype(jnp.bfloat16),
            value_heads,
            preferred_element_type=jnp.float32,
        )
        accum = accum * jnp.transpose(fade)[:, :, None] + added
        return (new_best, total, accum)

    def absorb(carry, piece):
        key_piece, value_piece, clip_piece = piece
        count = key_piece.shape[0]
        step_rows = next(
            (size_b for size_b in (512, 384, 256, 128) if count % size_b == 0 and count > size_b),
            count,
        )
        if step_rows == count:
            return absorb_block(carry, key_piece, value_piece, clip_piece)
        blocks = count // step_rows

        def scan_step(state, block_items):
            return (absorb_block(state, block_items[0], block_items[1], block_items[2]), None)

        stacked = (
            key_piece.reshape(blocks, step_rows, width),
            value_piece.reshape(blocks, step_rows, width),
            clip_piece.reshape(blocks, step_rows),
        )
        carry_out, unused = lax.scan(scan_step, carry, stacked)
        return carry_out

    start_state = (
        jnp.full((heads_here, slots), NEG_FILL, jnp.float32),
        jnp.zeros((heads_here, slots), jnp.float32),
        jnp.zeros((slots, heads_here, HEAD_DIM), jnp.float32),
    )
    best, total, accum = absorb(
        start_state,
        (
            lax.all_gather(keys[0], "seq", axis=0, tiled=True),
            lax.all_gather(values[0], "seq", axis=0, tiled=True),
            lax.all_gather(slot_clip, "seq", axis=0, tiled=True),
        ),
    )
    attended = (accum / jnp.transpose(total)[:, :, None]).reshape(slots, width)
    attended = jnp.where(live[:, None], attended, 0.0).astype(jnp.bfloat16)
    partial_out = jnp.dot(attended, w_out, preferred_element_type=jnp.float32)
    selector = (slot_clip[:, None] == jnp.arange(CLIPS, dtype=jnp.int32)[None, :]).astype(
        jnp.float32
    )
    row_mod = jnp.dot(
        selector, modulation.reshape(CLIPS, 4 * D), precision=lax.Precision.HIGHEST
    ).reshape(slots, 4, D)
    columns = D // lax.axis_size("blk")
    col_start = lax.axis_index("blk") * columns
    mod_cols = lax.dynamic_slice_in_dim(row_mod, col_start, columns, 2)
    projected = lax.psum(partial_out.astype(jnp.bfloat16), "blk").astype(jnp.float32)
    mixed = residual[0].astype(jnp.float32) + row_mod[:, 0] * projected
    centre = mixed - jnp.mean(mixed, axis=-1, keepdims=True)
    spread = jnp.mean(centre * centre, axis=-1, keepdims=True)
    normed = (centre * lax.rsqrt(spread + 1e-06) * (1.0 + row_mod[:, 2]) + row_mod[:, 1]).astype(
        jnp.bfloat16
    )
    mixed_cols = lax.dynamic_slice_in_dim(mixed, col_start, columns, 1)
    hidden = jax.nn.gelu(
        jnp.dot(normed, w_up, preferred_element_type=jnp.float32), approximate=True
    ).astype(jnp.bfloat16)
    terms = jnp.dot(hidden, w_down, preferred_element_type=jnp.float32)
    summed = lax.psum_scatter(
        terms.astype(jnp.bfloat16), "blk", scatter_dimension=1, tiled=True
    ).astype(jnp.float32)
    block_out = (mixed_cols + mod_cols[:, 3] * summed).astype(jnp.bfloat16)
    half_len = slots // 2
    side = lax.axis_index("cfg")
    partner = swapped(block_out, "cfg", 0)
    cond_all = jnp.where(side == 0, block_out, partner)
    uncond_all = jnp.where(side == 0, partner, block_out)
    cond_rows = lax.dynamic_slice_in_dim(cond_all, side * half_len, half_len, 0)
    uncond_rows = lax.dynamic_slice_in_dim(uncond_all, side * half_len, half_len, 0)
    clip_half = lax.dynamic_slice_in_dim(slot_clip, side * half_len, half_len, 0)
    clip_pick = (clip_half[:, None] == jnp.arange(CLIPS, dtype=jnp.int32)[None, :]).astype(
        jnp.float32
    )
    strength = jnp.sum(clip_pick * guide_scale[None, :], axis=1)
    cond_float = cond_rows.astype(jnp.float32)
    uncond_float = uncond_rows.astype(jnp.float32)
    guided = uncond_float + strength[:, None] * (cond_float - uncond_float)
    guided = jnp.where((clip_half < CLIPS)[:, None], guided, 0.0).astype(jnp.bfloat16)
    seq_count = lax.axis_size("seq")
    capacity = max(2, slots // seq_count)
    owner_half = lax.dynamic_slice_in_dim(owner[:, 0], side * half_len, half_len, 0)
    owner_hot = (owner_half[:, None] == jnp.arange(seq_count, dtype=jnp.int32)[None, :]).astype(
        jnp.int32
    )
    rank = jnp.sum((jnp.cumsum(owner_hot, axis=0) - owner_hot) * owner_hot, axis=1)
    target = owner_half * capacity + rank
    placing = (
        jnp.arange(seq_count * capacity, dtype=jnp.int32)[:, None] == target[None, :]
    ).astype(jnp.bfloat16)
    outgoing = jnp.dot(placing, guided, preferred_element_type=jnp.float32).astype(jnp.bfloat16)
    outgoing = outgoing.reshape(seq_count, capacity, columns)
    arrived = lax.all_to_all(outgoing, "seq", split_axis=0, concat_axis=0, tiled=True)
    return arrived.reshape(1, seq_count * capacity, columns)


def solution(mesh):
    placed = (
        P("cfg", "seq", "blk"),
        P("cfg", "seq", "blk"),
        P("cfg", "seq", "blk"),
        P("cfg", "seq", None),
        P("blk", None),
        P(None, "blk"),
        P("blk", None),
        P(),
        P(),
        P("seq"),
        P("seq", None),
    )
    return jax.shard_map(
        shards, mesh=mesh, in_specs=placed, out_specs=P("cfg", "seq", "blk"), check_vma=False
    )
```

profile of v0, /device:TPU:32, one launch (start us, length us, event | category | flops | bytes accessed | tf_op | source)
XLA Modules:
  0.0 713.3 jit_solution(6214231156440288934)
XLA Ops:
  10.8 48.8 %all-gather.2 = s32[32,1,384]{2,1,0:T(1,128)S(1)} all-gather(s32[1,1,384]{2,1,0:T(1,128)S(1)} %reshape.132), channel_id=1, replica_groups=mesh['cfg'=2,'seq'=32,'blk'=4] {'seq'}, dimensions={0}, use_global_device_ids=true | all-gather | bytes 50688 | tf_op jit(solution)/shard_map/all_gather | solution.py:88
  61.6 53.0 %all-gather.6.cloned.1.call-done = bf16[1,12288,384]{2,1,0:T(8,128)(2,1)} async-done(((bf16[1,384,384]{2,1,0:T(8,128)(2,1)}), bf16[1,12288,384]{2,1,0:T(8,128)(2,1)}) %all-gather.6.cloned.1.call-update) | async-done | bytes 9437200 | tf_op jit(solution)/shard_map/all_gather | solution.py:86
  114.6 103.2 %all-gather.8.cloned.1.call-done = bf16[1,12288,384]{2,1,0:T(8,128)(2,1)} async-done(((bf16[1,384,384]{2,1,0:T(8,128)(2,1)}), bf16[1,12288,384]{2,1,0:T(8,128)(2,1)}) %all-gather.8.cloned.1.call-update) | async-done | bytes 9437200 | tf_op jit(solution)/shard_map/all_gather | solution.py:87
  217.8 360.1 %while.15 = (s32[]{:T(128)}, f32[3,384]{1,0:T(4,128)S(1)}, f32[3,384]{1,0:T(4,128)}, f32[384,3,128]{0,2,1:T(8,128)}, s32[24,512]{1,0:T(8,128)}, /*index=5*/s32[3...) while((s32[]{:T(128)}, f32[3,384]{1,0:T(4,128)S(1)}, ...), condition=%wide.region_6.7_spmd.clone, body=%wide.region_3.6_spmd.clone.sunk | while | flops 309320448 | bytes 14176349 | solution.py:75
  228.6 2.7 fusion.94
  237.8 2.4 fusion.90
  243.4 2.9 fusion.94
  252.8 2.4 fusion.90
  258.4 2.9 fusion.94
  267.8 2.4 fusion.90
  273.4 2.9 fusion.94
  282.8 2.4 fusion.90
  288.4 2.9 fusion.94
  303.4 2.9 fusion.94
  312.8 2.4 fusion.90
  318.5 2.9 fusion.94
  327.9 2.4 fusion.90
  333.5 2.9 fusion.94
  342.9 2.4 fusion.90
  348.5 2.9 fusion.94
  363.5 2.9 fusion.94
  378.5 2.9 fusion.94
  393.5 2.9 fusion.94
  402.9 2.4 fusion.90
  408.5 2.9 fusion.94
  417.9 2.4 fusion.90
  423.6 2.9 fusion.94
  433.0 2.4 fusion.90
  438.6 2.9 fusion.94
  453.6 2.9 fusion.94
  468.6 2.9 fusion.94
  483.6 2.9 fusion.94
  493.0 2.4 fusion.90
  498.6 2.9 fusion.94
  508.0 2.4 fusion.90
  513.7 2.9 fusion.94
  523.1 2.4 fusion.90
  528.7 2.9 fusion.94
  538.1 2.4 fusion.90
  543.7 2.9 fusion.94
  558.7 2.9 fusion.94
  573.7 2.9 fusion.94
  581.7 6.4 fusion.56
  588.2 44.1 %all-reduce.3.cloned.1.call-done = bf16[384,1536]{1,0:T(8,128)(2,1)} async-done(((bf16[384,1536]{1,0:T(8,128)(2,1)}), bf16[384,1536]{1,0:T(8,128)(2,1)}) %all-reduce.3.cloned.1.call-update) | async-done | bytes 1179664 | tf_op jit(solution)/shard_map/psum | solution.py:103
  632.2 2.8 fusion.66
  635.4 10.1 %convolution_convert_fusion = bf16[384,1536]{1,0:T(8,128)(2,1)} fusion(bf16[1536,1536]{1,0:T(8,128)(2,1)} %param.19, bf16[1536,1536]{1,0:T(8,128)(2,1)} %param.18, f32[384,4,1536]{2,0,1:T(8,128)} %fusion.56, f32[384,1536]{1,0:T(8,128)S(1)} %get-tuple-element.158, f32[384]{0:T(512)S(1)} %add_rsqrt_fusion, f32[384]{0:T(512)S(1)} %broadcast_multiply_fusion), kind=kOutput, calls=%fused_computation.24 | convolution fusion | flops 3633315840 | bytes 17697792 | tf_op jit(solution)/shard_map/dot_general | solution.py:114
  652.9 22.6 %reduce-scatter.4.cloned.1.call-done = bf16[384,384]{1,0:T(8,128)(2,1)} async-done(((bf16[1536,384]{1,0:T(8,128)(2,1)}), bf16[384,384]{1,0:T(8,128)(2,1)}) %reduce-scatter.4.cloned.1.call-update) | async-done | bytes 294928
  680.8 25.2 %all_to_all.5 = bf16[32,12,384]{2,1,0:T(8,128)(2,1)S(1)} all-to-all(bf16[32,12,384]{2,1,0:T(8,128)(2,1)S(1)} %reshape.124), channel_id=1, replica_groups=mesh['cfg'=2,'seq'=32,'blk'=4] {'seq'}, dimensions={0} | all-to-all | bytes 589824 | tf_op jit(solution)/shard_map/all_to_all | solution.py:148
  (423 shorter events, 280.5 us)
Async XLA Ops:
  6.5 573.2 %copy-start = (bf16[384,1536]{1,0:T(8,128)(2,1)S(1)}, bf16[384,1536]{1,0:T(8,128)(2,1)}, u32[]{:S(2)}) copy-start(bf16[384,1536]{1,0:T(8,128)(2,1)} %param.17) | copy-start | bytes 3538948
  6.5 108.1 %all-gather.6.cloned.1.call-start = ((), (), s32[]{:S(2)}) async-start(), calls=%async_computation.3 | async-start | bytes 9732096 | tf_op jit(solution)/shard_map/all_gather | solution.py:86
  7.3 210.5 %all-gather.8.cloned.1.call-start = ((), (), s32[]{:S(2)}) async-start(), calls=%async_computation.4 | async-start | bytes 9732096 | tf_op jit(solution)/shard_map/all_gather | solution.py:87
  8.0 624.2 %all-reduce.3.cloned.1.call-start = ((), (), s32[]{:S(2)}) async-start(), calls=%async_computation.2 | async-start | bytes 2359296 | tf_op jit(solution)/shard_map/psum | solution.py:103
  228.6 2.7 copy-start.1
  231.3 0.7 copy-start.2
  243.4 2.9 copy-start.1
  246.3 0.7 copy-start.2
  258.4 2.9 copy-start.1
  261.3 0.7 copy-start.2
  273.4 2.9 copy-start.1
  276.3 0.7 copy-start.2
  288.4 2.9 copy-start.1
  291.3 0.7 copy-start.2
  303.4 2.9 copy-start.1
  306.4 0.7 copy-start.2
  318.5 2.9 copy-start.1
  321.4 0.7 copy-start.2
  333.5 2.9 copy-start.1
  336.4 0.7 copy-start.2
  348.5 2.9 copy-start.1
  351.4 0.7 copy-start.2
  363.5 2.9 copy-start.1
  366.4 0.7 copy-start.2
  378.5 2.9 copy-start.1
  393.5 2.9 copy-start.1
  408.5 2.9 copy-start.1
  423.6 2.9 copy-start.1
  438.6 2.9 copy-start.1
  441.5 0.7 copy-start.2
  453.6 2.9 copy-start.1
  456.5 0.7 copy-start.2
  468.6 2.9 copy-start.1
  483.6 2.9 copy-start.1
  498.6 2.9 copy-start.1
  513.7 2.9 copy-start.1
  528.7 2.9 copy-start.1
  531.6 0.7 copy-start.2
  543.7 2.9 copy-start.1
  546.6 0.7 copy-start.2
  558.7 2.9 copy-start.1
  573.7 2.9 copy-start.1
  579.0 2.6 copy-start.4
  579.1 2.6 copy-start.5
  581.6 93.9 %reduce-scatter.4.cloned.1.call-start = ((), (), s32[]{:S(2)}) async-start(), calls=%async_computation.5 | async-start | bytes 1474560
  645.5 2.4 copy-start.6
  652.9 27.4 %copy-start.7 = (pred[192]{0:T(512)(128)(4,1)S(1)}, pred[192]{0:T(512)(128)(4,1)}, u32[]{:S(2)}) copy-start(pred[192]{0:T(512)(128)(4,1)} %get-tuple-element.155) | copy-start | bytes 580
  678.7 1.7 collective-permute-start
  (34 other events, 21.3 us)
Sparse Core Ops, SparseCore 0:
  9.9 104.6 all-gather.5
  117.2 100.5 all-gather.7
  581.8 50.4 all-reduce.2
  648.0 27.5 reduce-scatter.3
where the time goes:
time: 720 us; the launch traced here: 713 us
  waiting for transfers between devices  225 us (31%)
  local copies, waits for them, and re-layouts  160 us (22%)
  matrix products  146 us (20%)
  other arithmetic  94.2 us (13%)
  blocking collectives  74 us (10%)
  between operations  13.3 us (2%)
    dynamic_slice x96, local copies, waits for them, and re-layouts, absorb(): carry_out, unused = lax.scan(scan_step, carry, stacked)  133 us
    all_gather x1, waiting for transfers between devices, shards(): lax.all_gather(values[0], 'seq', axis=0, tiled=True)  103 us
    dot_general x24, matrix products, absorb_block(): jnp.einsum('hqk,khd->qhd', probs.astype(jnp.bfloat16), value_heads, prefe...  69.4 us
    dot_general x24, matrix products, absorb_block(): jnp.einsum('qhd,khd->hqk', query_heads, key_heads, preferred_element_type...  57.5 us
    all_gather x1, waiting for transfers between devices, shards(): lax.all_gather(keys[0], 'seq', axis=0, tiled=True)  53 us
    all_gather x1, blocking collectives, shards(): lax.all_gather(slot_clip, 'seq', axis=0, tiled=True)  48.8 us
    psum x1, waiting for transfers between devices, shards(): lax.psum(partial_out.astype(jnp.bfloat16), 'blk').astype(jnp.float32)  44.1 us
    and x24, other arithmetic, absorb_block(): kept = (clip_block[None, :] == slot_clip[:, None]) & live[:, None]  37.3 us
  transfers between devices with their start and end apart: 5, of which 5 were waited for; matrix products, arithmetic and copies ran while one was open for 2% of the time, Pallas kernels for 0%

commit v1 on v0

v1 whole, which is shorter than its diff:
```python
import functools
import math

import jax
import jax.numpy as jnp
from jax import lax
from jax.experimental import pallas as pl
from jax.experimental.pallas import tpu as pltpu
from jax.sharding import PartitionSpec as P

D = 1536
HEAD_DIM = 128
CLIPS = 3
HEADS_HERE = 3
GROUP = 128
Y, Z = 4, 8
MSG = 400
KV = pl.ds(128, 272)
NEG_FILL = -1e30
EXP2_SCALE = math.log2(math.e) / math.sqrt(HEAD_DIM)
MESH = pl.DeviceIdType.MESH
NEAR_FIRST = (1, 7, 2, 6, 3, 5, 4)


def swapped(value, axis, bit):
    mask = 2**bit
    pairs = [(source, source ^ mask) for source in range(lax.axis_size(axis))]
    return lax.ppermute(value, axis, pairs)


def remote(src, dst, send, recv, seq):
    return pltpu.make_async_remote_copy(
        src_ref=src,
        dst_ref=dst,
        send_sem=send,
        recv_sem=recv,
        device_id={"seq": seq},
        device_id_type=MESH,
    )


def attend_tile(query, kv, best, total, accum):
    keys = kv[:, 128:256, :].reshape(8 * GROUP, HEAD_DIM)
    scores = lax.dot_general(
        query, keys, (((1,), (1,)), ((), ())), preferred_element_type=jnp.float32
    )
    pieces = []
    for i in range(8):
        bias = kv[i, 384:400, :].astype(jnp.float32)[0:1]
        pieces.append(scores[:, i * GROUP : (i + 1) * GROUP] + bias)
    peak = functools.reduce(jnp.maximum, pieces)
    new_best = jnp.maximum(best, jnp.max(peak, axis=1, keepdims=True))
    probs = [jnp.exp2((piece - new_best) * EXP2_SCALE) for piece in pieces]
    fade = jnp.exp2((best - new_best) * EXP2_SCALE)
    total = total * fade + functools.reduce(jnp.add, probs)
    weights = jnp.concatenate([prob.astype(jnp.bfloat16) for prob in probs], axis=1)
    values = kv[:, 256:384, :].reshape(8 * GROUP, HEAD_DIM)
    accum = accum * fade + jnp.dot(weights, values, preferred_element_type=jnp.float32)
    return new_best, total, accum


def attention_kernel(
    perm_ref,
    q_ref,
    k_ref,
    v_ref,
    bias_ref,
    att_ref,
    stage,
    buf,
    kv9,
    q9,
    part_out,
    part_in,
    best_s,
    total_s,
    accum_s,
    out_stage,
    zsend,
    zrecv,
    rsend,
    rrecv,
    ysend,
    yrecv,
    qsend,
    qrecv,
    psend,
    precv,
    osend,
    orecv,
):
    me = lax.axis_index("seq")
    y, z = me // Z, me % Z
    right = ((y + 1) % Y) * Z + z
    left = ((y + 3) % Y) * Z + z
    across = ((y + 2) % Y) * Z + z

    def along(t):
        return y * Z + (z + t) % Z

    barrier = pltpu.get_barrier_semaphore()
    for t in range(1, Z):
        pl.semaphore_signal(barrier, inc=1, device_id={"seq": along(t)}, device_id_type=MESH)
    for peer in (right, left, across):
        pl.semaphore_signal(barrier, inc=1, device_id={"seq": peer}, device_id_type=MESH)

    for which, ref in enumerate((q_ref, k_ref, v_ref)):
        rows = jnp.dot(perm_ref[...], ref[...], preferred_element_type=jnp.float32)
        rows = rows.astype(jnp.bfloat16)
        for h in range(HEADS_HERE):
            for c in range(CLIPS):
                stage[3 * h + c, which * 128 : which * 128 + 128, :] = rows[
                    c * 128 : c * 128 + 128, h * 128 : h * 128 + 128
                ]
    for h in range(HEADS_HERE):
        for c in range(CLIPS):
            stage[3 * h + c, 384:400, :] = bias_ref[c]

    pl.semaphore_wait(barrier, Z - 1 + 3)

    sends = []
    for t in NEAR_FIRST:
        copy = remote(
            stage.at[(z + t) % Z], buf.at[0, t], zsend.at[t], zrecv.at[t], along(t)
        )
        copy.start()
        sends.append(copy)
    ring = {
        1: remote(stage.at[8, KV], kv9.at[1, KV], rsend.at[1], rrecv.at[1], along(1)),
        7: remote(stage.at[8, KV], kv9.at[7, KV], rsend.at[7], rrecv.at[7], along(7)),
    }
    for copy in ring.values():
        copy.start()
    for j, peer in ((1, right), (2, left), (3, across)):
        copy = remote(stage.at[8, pl.ds(0, 128)], q9.at[j], qsend.at[j], qrecv.at[j], peer)
        copy.start()
        sends.append(copy)

    def pass_on(t):
        for j, peer in ((1, right), (2, left)):
            copy = remote(
                buf.at[0, t, KV], buf.at[j, t, KV], ysend.at[j - 1, t], yrecv.at[j - 1, t], peer
            )
            copy.start()
            sends.append(copy)

    buf[0, 0] = stage[z]
    pass_on(0)
    kv9[0] = stage[8]
    q9[0] = stage[8, 0:128, :]
    best_s[...] = jnp.full_like(best_s, NEG_FILL)
    total_s[...] = jnp.zeros_like(total_s)
    accum_s[...] = jnp.zeros_like(accum_s)

    def relay(t, onto, peer):
        ring[t].wait_recv()
        ring[onto] = remote(
            kv9.at[t, KV], kv9.at[onto, KV], rsend.at[onto], rrecv.at[onto], peer
        )
        ring[onto].start()

    for i, t in enumerate(NEAR_FIRST):
        sends[i].wait_recv()
        pass_on(t)
        if i == 1:
            relay(1, 2, along(1))
            relay(7, 6, along(7))
        if i == 3:
            relay(2, 3, along(1))
            relay(6, 5, along(7))
        if i == 5:
            relay(3, 4, along(1))
    ring[5].wait_recv()
    ring[4].wait_recv()
    for j in (1, 2, 3):
        sends[6 + j].wait_recv()

    def ninth(tile, carry):
        query = q9[pl.ds(2 * tile, 2)].reshape(256, HEAD_DIM)
        zero = jnp.zeros((256, HEAD_DIM), jnp.float32)
        best, total, accum = attend_tile(query, kv9, zero + NEG_FILL, zero, zero)
        total = jnp.sum(total, axis=1, keepdims=True)
        lane = lax.broadcasted_iota(jnp.int32, (256, HEAD_DIM), 1)
        stats = jnp.where(lane < 64, best, total)
        part_out[pl.ds(2 * tile, 2), :, 0:128] = accum.reshape(2, 128, 128)
        part_out[pl.ds(2 * tile, 2), :, 128:256] = stats.reshape(2, 128, 128)
        return carry

    lax.fori_loop(0, 2, ninth, 0)
    parts = []
    for j, onto, peer in ((1, 2, left), (2, 1, right), (3, 3, across)):
        copy = remote(part_out.at[j], part_in.at[onto], psend.at[j], precv.at[onto], peer)
        copy.start()
        parts.append(copy)

    def out_block(problem):
        row = pl.multiple_of((problem % 3) * 128, 128)
        column = pl.multiple_of((problem // 3) * 128, 128)
        return att_ref.at[pl.ds(row, 128), pl.ds(column, 128)]

    def group(j, carry):
        @pl.when(j == 1)
        def _():
            for t in range(Z):
                for side, peer in ((0, right), (1, left)):
                    remote(
                        buf.at[0, t, KV], buf.at[1 + side, t, KV],
                        ysend.at[side, t], yrecv.at[side, t], peer,
                    ).wait_recv()
                    if t % 2 == side:
                        remote(
                            buf.at[1 + side, t, KV], buf.at[3, t, KV],
                            ysend.at[2, t], yrecv.at[2, t], peer,
                        ).start()

        @pl.when(j == 3)
        def _():
            for t in range(Z):
                remote(
                    buf.at[1 + t % 2, t, KV], buf.at[3, t, KV],
                    ysend.at[2, t], yrecv.at[2, t], (right, left)[t % 2],
                ).wait()

        def one(tile, inner):
            rows = pl.ds(pl.multiple_of(tile * 256, 256), 256)
            query = buf[0, pl.ds(2 * tile, 2), 0:128, :].reshape(256, HEAD_DIM)
            best, total, accum = attend_tile(
                query, buf.at[j], best_s[rows, :], total_s[rows, :], accum_s[rows, :]
            )
            best_s[rows, :] = best
            total_s[rows, :] = total
            accum_s[rows, :] = accum

            @pl.when(j == 3)
            def _():
                result = accum / jnp.sum(total, axis=1, keepdims=True)
                out_stage[pl.ds(2 * tile, 2)] = result.astype(jnp.bfloat16).reshape(2, 128, 128)

                @pl.when(tile == 0)
                def _():
                    pltpu.make_async_copy(out_stage.at[0], out_block(z), osend.at[0]).start()

                @pl.when(tile > 0)
                def _():
                    t = 2 * tile
                    remote(
                        out_stage.at[t], out_block(z), osend.at[t], orecv.at[t],
                        y * Z + (z + Z - t) % Z,
                    ).start()

                t = 2 * tile + 1
                remote(
                    out_stage.at[t], out_block(z), osend.at[t], orecv.at[t],
                    y * Z + (z + Z - t) % Z,
                ).start()

            return inner

        return lax.fori_loop(0, 4, one, carry)

    lax.fori_loop(0, 4, group, 0)

    for copy in parts:
        copy.wait()
    pieces = [part_out.at[0], part_in.at[1], part_in.at[2], part_in.at[3]]
    bests = [piece[:, 128:129] for piece in pieces]
    top = functools.reduce(jnp.maximum, bests)
    weights = [jnp.exp2((best - top) * EXP2_SCALE) for best in bests]
    total = functools.reduce(
        jnp.add, [weight * piece[:, 192:193] for weight, piece in zip(weights, pieces)]
    )
    accum = functools.reduce(
        jnp.add, [weight * piece[:, 0:128] for weight, piece in zip(weights, pieces)]
    )
    att_ref[256:384, 256:384] = (accum / total).astype(jnp.bfloat16)

    pltpu.make_async_copy(out_stage.at[0], out_block(z), osend.at[0]).wait()
    for t in range(1, Z):
        copy = remote(
            out_stage.at[t], out_block((z + t) % Z), osend.at[t], orecv.at[t], along(Z - t)
        )
        copy.wait()
    for copy in sends:
        copy.wait_send()
    for copy in ring.values():
        copy.wait_send()


def attention(perm, queries, keys, values, bias):
    dma = pltpu.SemaphoreType.DMA
    vmem = pltpu.VMEM
    return pl.pallas_call(
        attention_kernel,
        out_shape=jax.ShapeDtypeStruct((384, 384), jnp.bfloat16),
        in_specs=[pl.BlockSpec(memory_space=vmem)] * 5,
        out_specs=pl.BlockSpec(memory_space=vmem),
        scratch_shapes=[
            vmem((9, MSG, 128), jnp.bfloat16),
            vmem((4, Z, MSG, 128), jnp.bfloat16),
            vmem((Z, MSG, 128), jnp.bfloat16),
            vmem((4, 128, 128), jnp.bfloat16),
            vmem((4, 128, 256), jnp.float32),
            vmem((4, 128, 256), jnp.float32),
            vmem((1024, 128), jnp.float32),
            vmem((1024, 128), jnp.float32),
            vmem((1024, 128), jnp.float32),
            vmem((Z, 128, 128), jnp.bfloat16),
            dma((Z,)),
            dma((Z,)),
            dma((Z,)),
            dma((Z,)),
            dma((3, Z)),
            dma((3, Z)),
            dma((4,)),
            dma((4,)),
            dma((4,)),
            dma((4,)),
            dma((Z,)),
            dma((Z,)),
        ],
        compiler_params=pltpu.CompilerParams(
            collective_id=0, has_side_effects=True, vmem_limit_bytes=40 * 2**20
        ),
        name="clip_attention",
    )(perm, queries, keys, values, bias)


def clip_order(slot_clip):
    slots = slot_clip.shape[0]
    first = slot_clip[0]
    live_count = jnp.sum((slot_clip < CLIPS).astype(jnp.int32))
    row = jnp.arange(slots, dtype=jnp.int32)
    clip, rank = row // GROUP, row % GROUP
    slot_of = 3 * rank + (clip + 6 - first) % 3
    return slot_of, slot_of < live_count


def shards(
    queries, keys, values, residual, w_out, w_up, w_down, modulation, guide_scale, slot_clip, owner
):
    slots = slot_clip.shape[0]
    slot_of, live = clip_order(slot_clip)
    perm = (slot_of[:, None] == jnp.arange(slots, dtype=jnp.int32)[None, :]).astype(jnp.bfloat16)
    bias = jnp.broadcast_to(
        jnp.where(live, 0.0, NEG_FILL).astype(jnp.bfloat16).reshape(CLIPS, 1, GROUP),
        (CLIPS, 16, GROUP),
    )
    attended = attention(perm, queries[0], keys[0], values[0], bias)
    partial_out = jnp.dot(attended, w_out, preferred_element_type=jnp.float32)
    mod = jnp.repeat(modulation, GROUP, axis=0)
    columns = D // lax.axis_size("blk")
    col_start = lax.axis_index("blk") * columns
    gate_mlp = lax.dynamic_slice_in_dim(mod[:, 3], col_start, columns, 1)
    stream = jnp.dot(perm, residual[0], preferred_element_type=jnp.float32)
    projected = lax.psum(partial_out.astype(jnp.bfloat16), "blk").astype(jnp.float32)
    mixed = stream + mod[:, 0] * projected
    centre = mixed - jnp.mean(mixed, axis=-1, keepdims=True)
    spread = jnp.mean(centre * centre, axis=-1, keepdims=True)
    normed = (centre * lax.rsqrt(spread + 1e-06) * (1.0 + mod[:, 2]) + mod[:, 1]).astype(
        jnp.bfloat16
    )
    mixed_cols = lax.dynamic_slice_in_dim(mixed, col_start, columns, 1)
    hidden = jax.nn.gelu(
        jnp.dot(normed, w_up, preferred_element_type=jnp.float32), approximate=True
    ).astype(jnp.bfloat16)
    terms = jnp.dot(hidden, w_down, preferred_element_type=jnp.float32)
    summed = lax.psum_scatter(
        terms.astype(jnp.bfloat16), "blk", scatter_dimension=1, tiled=True
    ).astype(jnp.float32)
    block_out = (mixed_cols + gate_mlp * summed).astype(jnp.bfloat16)

    side = lax.axis_index("cfg")
    half_group = GROUP // 2
    split = block_out.reshape(CLIPS, 2, half_group, columns)
    mine = lax.dynamic_index_in_dim(split, side, 1, keepdims=False)
    partner = swapped(lax.dynamic_index_in_dim(split, 1 - side, 1, keepdims=False), "cfg", 0)
    cond = jnp.where(side == 0, mine, partner).astype(jnp.float32)
    uncond = jnp.where(side == 0, partner, mine).astype(jnp.float32)
    guided = uncond + guide_scale[:, None, None] * (cond - uncond)
    live_half = lax.dynamic_index_in_dim(live.reshape(CLIPS, 2, half_group), side, 1, keepdims=False)
    guided = jnp.where(live_half[:, :, None], guided, 0.0).astype(jnp.bfloat16)
    guided = guided.reshape(slots // 2, columns)

    seq_count = lax.axis_size("seq")
    capacity = max(2, slots // seq_count)
    half_len = slots // 2
    owner_half = lax.dynamic_slice_in_dim(owner[:, 0], side * half_len, half_len, 0)
    place = jnp.arange(half_len, dtype=jnp.int32)
    earlier = (owner_half[:, None] == owner_half[None, :]) & (place[None, :] < place[:, None])
    rank = jnp.sum(earlier.astype(jnp.int32), axis=1)
    target = owner_half * capacity + rank
    slot_half = lax.dynamic_index_in_dim(
        slot_of.reshape(CLIPS, 2, half_group), side, 1, keepdims=False
    ).reshape(half_len) - side * half_len
    target = jnp.sum(
        jnp.where(slot_half[:, None] == place[None, :], target[None, :], 0), axis=1
    )
    placing = (
        jnp.arange(seq_count * capacity, dtype=jnp.int32)[:, None] == target[None, :]
    ).astype(jnp.bfloat16)
    outgoing = jnp.dot(placing, guided, preferred_element_type=jnp.float32).astype(jnp.bfloat16)
    outgoing = outgoing.reshape(seq_count, capacity, columns)
    arrived = lax.all_to_all(outgoing, "seq", split_axis=0, concat_axis=0, tiled=True)
    return arrived.reshape(1, seq_count * capacity, columns)


def solution(mesh):
    placed = (
        P("cfg", "seq", "blk"),
        P("cfg", "seq", "blk"),
        P("cfg", "seq", "blk"),
        P("cfg", "seq", None),
        P("blk", None),
        P(None, "blk"),
        P("blk", None),
        P(),
        P(),
        P("seq"),
        P("seq", None),
    )
    return jax.shard_map(
        shards, mesh=mesh, in_specs=placed, out_specs=P("cfg", "seq", "blk"), check_vma=False
    )
```

time: 720 us -> 213 us (0.30)
  waiting for transfers between devices: 225 us -> 72.3 us
  local copies, waits for them, and re-layouts: 160 us -> 18.2 us
  matrix products: 146 us -> 14.3 us
  other arithmetic: 94.2 us -> 7.76 us
  Pallas kernels: 0 us -> 60.7 us
  blocking collectives: 74 us -> 25.2 us
    all_gather x2 -> x0, waiting for transfers between devices: 156 us -> none  [the longest x1 103 us: shards(): lax.all_gather(values[0], 'seq', axis=0, tiled=True)]
    dynamic_slice x96 -> x0, local copies, waits for them, and re-layouts: 133 us -> none  [absorb(): carry_out, unused = lax.scan(scan_step, carry, stacked)]
    dot_general x49 -> x1, matrix products: 133 us -> 0.97 us  [shards(): stream = jnp.dot(perm, residual[0], preferred_element_type=jnp.float32)]
    pallas_call x0 -> x1, Pallas kernels: none -> 60.7 us  [attention(): pl.pallas_call(attention_kernel, out_shape=jax.ShapeDtypeStruct((384, 384...]
    all_gather x1 -> x0, blocking collectives: 48.8 us -> none  [shards(): lax.all_gather(slot_clip, 'seq', axis=0, tiled=True)]
    and x24 -> x0, other arithmetic: 37.3 us -> none  [absorb_block(): kept = (clip_block[None, :] == slot_clip[:, None]) & live[:, None]]
    transpose x24 -> x0, other arithmetic: 31.1 us -> none  [absorb_block(): accum = accum * jnp.transpose(fade)[:, :, None] + added]
    while x168 -> x0, local copies, waits for them, and re-layouts: 17.8 us -> none
  transfers between devices with their start and end apart: 5 -> 3, of which waited for: 5 -> 3; matrix products, arithmetic and copies ran while one was open for 2% -> 2% of each run, Pallas kernels for 0% -> 0%
where the time goes in v1:
time: 213 us; the launch traced here: 212 us
  waiting for transfers between devices  72.3 us (34%)
  Pallas kernels  60.7 us (28%)
  blocking collectives  25.2 us (12%)
  local copies, waits for them, and re-layouts  18.2 us (9%)
  matrix products  14.3 us (7%)
  between operations  13.6 us (6%)
  other arithmetic  7.76 us (4%)
    pallas_call x1, Pallas kernels, attention(): pl.pallas_call(attention_kernel, out_shape=jax.ShapeDtypeStruct((384, 384...  60.7 us
    psum x1, waiting for transfers between devices, shards(): lax.psum(partial_out.astype(jnp.bfloat16), 'blk').astype(jnp.float32)  48.3 us
    all_to_all x1, blocking collectives, shards(): lax.all_to_all(outgoing, 'seq', split_axis=0, concat_axis=0, tiled=True)  25.2 us
    unnamed x3, waiting for transfers between devices  23.5 us
    unnamed x23, local copies, waits for them, and re-layouts  11.5 us
    dot_general x1, matrix products, shards(): terms = jnp.dot(hidden, w_down, preferred_element_type=jnp.float32)  10 us
  transfers between devices with their start and end apart: 3, of which 3 were waited for; matrix products, arithmetic and copies ran while one was open for 2% of the time, Pallas kernels for 0%

profile of v1, /device:TPU:32, one launch (start us, length us, event | category | flops | bytes accessed | tf_op | source)
XLA Modules:
  0.0 212.2 jit_solution(14300476458616465787)
XLA Ops:
  6.5 0.0 copy-start
  6.5 0.0 all-reduce.2.cloned.1.call-start
  6.5 1.3 slice.15
  7.8 1.3 convert_reduce_fusion.1
  9.2 0.7 fusion.41
  9.8 0.1 fusion.25.perm_ref
  10.0 1.3 select_convert_fusion
  11.3 0.0 copy-start.1
  11.3 1.0 copy-done.1
  12.2 1.0 copy-done.2
  13.2 1.0 copy-done.3
  14.1 60.7 %clip_attention.1 = bf16[384,384]{1,0:T(8,128)(2,1)S(1)} custom-call(bf16[384,384]{1,0:T(8,128)(2,1)S(1)} %fusion.25.perm_ref, bf16[384,384]{1,0:T(8,128)(2,1)S(1)} %bitcast.67, bf16[384,384]{1,0:T(8,128)(2,1)S(1)} %bitcast.68, bf16[384,384]{1,0:T(8,128)(2,1)S(1)} %bitcast.69, bf16[3,16,128]{2,1,0:T(8,128)(2,1)S(1)} %broadcast_in_dim.64.bias_ref), custom_call_target="tpu_custom_call" | custom-call | tf_op jit(solution)/shard_map/clip_attention/pallas_call | solution.py:292
  74.8 3.1 %convolution_convert_fusion.1 = bf16[384,1536]{1,0:T(8,128)(2,1)} fusion(bf16[384,384]{1,0:T(8,128)(2,1)S(1)} %clip_attention.1, bf16[384,1536]{1,0:T(8,128)(2,1)} %param.15), kind=kOutput, calls=%fused_computation.3 | convolution fusion | flops 453574656 | bytes 2654208 | tf_op jit(solution)/shard_map/dot_general | solution.py:349
  77.9 0.0 all-reduce.2.cloned.1.call-update
  77.9 0.0 reduce-scatter.4.cloned.1.call-start
  78.0 0.0 copy-done.7
  78.0 48.3 %all-reduce.2.cloned.1.call-done = bf16[384,1536]{1,0:T(8,128)(2,1)} async-done(((bf16[384,1536]{1,0:T(8,128)(2,1)}), bf16[384,1536]{1,0:T(8,128)(2,1)}) %all-reduce.2.cloned.1.call-update) | async-done | bytes 1179664 | tf_op jit(solution)/shard_map/psum | solution.py:355
  126.4 1.2 broadcast_in_dim.61
  127.5 0.0 copy-start.4
  127.6 3.6 %copy-done.4 = f32[3,128,4,1536]{3,1,0,2:T(8,128)} copy-done((f32[3,128,4,1536]{3,1,0,2:T(8,128)}, f32[3,128,4,1536]{3,1,0,2:T(8,128)S(1)}, u32[]{:S(2)}) %copy-start.4) | copy-done | bytes 9437208
  131.2 0.0 copy-done
  131.2 0.0 copy-done.6
  131.2 1.0 fusion.63
  132.2 0.4 multiply_reduce_fusion
  132.5 10.0 %convolution_convert_fusion = bf16[384,1536]{1,0:T(8,128)(2,1)} fusion(bf16[1536,1536]{1,0:T(8,128)(2,1)} %param.17, bf16[1536,1536]{1,0:T(8,128)(2,1)} %param.16, f32[384,4,1536]{2,0,1:T(8,128)} %bitcast.71, f32[384,1536]{1,0:T(8,128)S(1)} %get-tuple-element.6, f32[384]{0:T(512)S(1)} %add_rsqrt_fusion, f32[384]{0:T(512)S(1)} %broadcast_multiply_fusion), kind=kOutput, calls=%fused_computation.2 | convolution fusion | flops 3633315840 | bytes 17697792 | tf_op jit(solution)/shard_map/dot_general | solution.py:366
  142.6 2.4 %copy.16 = bf16[384,1536]{0,1:T(8,128)(2,1)} copy(bf16[384,1536]{1,0:T(8,128)(2,1)} %convolution_convert_fusion) | data formatting | bytes 2359296
  145.0 0.0 reduce-scatter.4.cloned.1.call-update
  145.0 0.0 copy-start.8
  145.0 3.2 %slice.21 = f32[384,1,1536]{2,0,1:T(8,128)} slice(f32[384,4,1536]{2,0,1:T(8,128)} %bitcast.72), slice={[0:384], [3:4], [0:1536]} | slice | bytes 4718592 | tf_op jit(solution)/shard_map/slice | solution.py:353
  148.2 0.0 copy-done.8
  148.2 0.1 constant_dynamic-slice_fusion
  148.3 0.7 fusion.33
  149.0 0.2 convert_reduce_fusion
  149.2 23.5 %reduce-scatter.4.cloned.1.call-done = bf16[384,384]{1,0:T(8,128)(2,1)} async-done(((bf16[1536,384]{1,0:T(8,128)(2,1)}), bf16[384,384]{1,0:T(8,128)(2,1)}) %reduce-scatter.4.cloned.1.call-update) | async-done | bytes 294928
  172.7 1.8 copy.17
  174.5 1.3 fusion.24
  175.8 0.0 copy-start.5
  175.8 0.7 copy-done.5
  176.5 0.1 collective-permute-start
  176.6 0.6 compare_bitcast_fusion
  177.3 0.1 sub.66
  177.4 0.2 select_reduce_fusion
  177.5 0.5 collective-permute-done
  178.0 1.0 fusion.28
  179.0 0.3 convolution_convert_fusion.2
  179.3 0.1 reshape.160
  179.4 25.2 %all_to_all.5 = bf16[32,12,384]{2,1,0:T(8,128)(2,1)S(1)} all-to-all(bf16[32,12,384]{2,1,0:T(8,128)(2,1)S(1)} %reshape.160), channel_id=1, replica_groups=mesh['cfg'=2,'seq'=32,'blk'=4] {'seq'}, dimensions={0} | all-to-all | bytes 589824 | tf_op jit(solution)/shard_map/all_to_all | solution.py:403
  204.6 0.8 reshape.161
  (13 shorter events, 0.1 us)
Async XLA Ops:
  6.5 124.6 %copy-start = (bf16[1,384,1536]{2,1,0:T(8,128)(2,1)S(1)}, bf16[1,384,1536]{2,1,0:T(8,128)(2,1)}, u32[]{:S(2)}) copy-start(bf16[1,384,1536]{2,1,0:T(8,128)(2,1)} %param.14) | copy-start | bytes 3538948
  6.5 119.8 %all-reduce.2.cloned.1.call-start = ((), (), s32[]{:S(2)}) async-start(), calls=%async_computation.2 | async-start | bytes 2359296 | tf_op jit(solution)/shard_map/psum | solution.py:355
  11.3 1.0 copy-start.1
  12.2 1.0 copy-start.2
  13.2 1.0 copy-start.3
  14.1 63.8 %copy-start.7 = (f32[3,4,1536]{2,1,0:T(4,128)S(1)}, f32[3,4,1536]{2,1,0:T(4,128)}, u32[]{:S(2)}) copy-start(f32[3,4,1536]{2,1,0:T(4,128)} %param.18) | copy-start | bytes 221188
  77.9 94.8 %reduce-scatter.4.cloned.1.call-start = ((), (), s32[]{:S(2)}) async-start(), calls=%async_computation.3 | async-start | bytes 1474560
  126.4 4.8 %copy-start.6 = (bf16[384,1536]{1,0:T(8,128)(2,1)S(1)}, bf16[384,1536]{1,0:T(8,128)(2,1)}, u32[]{:S(2)}) copy-start(bf16[384,1536]{1,0:T(8,128)(2,1)} %all-reduce.2.cloned.1.call-done) | copy-start | bytes 3538948
  127.5 3.6 %copy-start.4 = (f32[3,128,4,1536]{3,1,0,2:T(8,128)}, f32[3,128,4,1536]{3,1,0,2:T(8,128)S(1)}, u32[]{:S(2)}) copy-start(f32[3,128,4,1536]{3,1,0,2:T(8,128)S(1)} %broadcast_in_dim.61) | copy-start | bytes 28311556
  145.0 3.2 %copy-start.8 = (s32[384,1]{0,1:T(1,128)S(1)}, s32[384,1]{0,1:T(1,128)}, u32[]{:S(2)}) copy-start(s32[384,1]{0,1:T(1,128)} %param.21) | copy-start | bytes 4612
  148.2 29.8 %copy-start.9 = (f32[3]{0:T(128)S(1)}, f32[3]{0:T(128)}, u32[]{:S(2)}) copy-start(f32[3]{0:T(128)} %param.19) | copy-start | bytes 40
  175.8 0.7 copy-start.5
  176.5 1.5 collective-permute-start
Sparse Core Ops, SparseCore 0:
  78.0 48.2 all-reduce.1
  145.1 27.5 reduce-scatter.3

commit v2 on v1

v2 whole, which is shorter than its diff:
```python
import functools
import math

import jax
import jax.numpy as jnp
from jax import lax
from jax.experimental import pallas as pl
from jax.experimental.pallas import tpu as pltpu
from jax.sharding import PartitionSpec as P

D = 1536
HEAD_DIM = 128
CLIPS = 3
HEADS_HERE = 3
GROUP = 128
Y, Z = 4, 8
MSG = 400
KV = pl.ds(128, 272)
NEG_FILL = -1e30
EXP2_SCALE = math.log2(math.e) / math.sqrt(HEAD_DIM)
MESH = pl.DeviceIdType.MESH
NEAR_FIRST = (1, 7, 2, 6, 3, 5, 4)
X = 4
SLOTS = 384
HALF = 192
CAP = 12
TOP, LOW = pl.ds(0, HALF), pl.ds(HALF, HALF)


def remote(src, dst, send, recv, peer):
    return pltpu.make_async_remote_copy(
        src_ref=src,
        dst_ref=dst,
        send_sem=send,
        recv_sem=recv,
        device_id=peer,
        device_id_type=MESH,
    )


def attend_tile(query, kv, best, total, accum):
    keys = kv[:, 128:256, :].reshape(8 * GROUP, HEAD_DIM)
    scores = lax.dot_general(
        query, keys, (((1,), (1,)), ((), ())), preferred_element_type=jnp.float32
    )
    pieces = []
    for i in range(8):
        bias = kv[i, 384:400, :].astype(jnp.float32)[0:1]
        pieces.append(scores[:, i * GROUP : (i + 1) * GROUP] + bias)
    peak = functools.reduce(jnp.maximum, pieces)
    new_best = jnp.maximum(best, jnp.max(peak, axis=1, keepdims=True))
    probs = [jnp.exp2((piece - new_best) * EXP2_SCALE) for piece in pieces]
    fade = jnp.exp2((best - new_best) * EXP2_SCALE)
    total = total * fade + functools.reduce(jnp.add, probs)
    weights = jnp.concatenate([prob.astype(jnp.bfloat16) for prob in probs], axis=1)
    values = kv[:, 256:384, :].reshape(8 * GROUP, HEAD_DIM)
    accum = accum * fade + jnp.dot(weights, values, preferred_element_type=jnp.float32)
    return new_best, total, accum


def block_kernel(
    clip_ref,
    owner_ref,
    guide_ref,
    q_hbm,
    k_hbm,
    v_hbm,
    res_hbm,
    mod_hbm,
    w_out_hbm,
    w_up_hbm,
    w_down_hbm,
    out_ref,
    qkv,
    perm,
    stage,
    buf,
    kv9,
    q9,
    part_out,
    part_in,
    best_s,
    total_s,
    accum_s,
    out_stage,
    att,
    w_out,
    w_up,
    w_down,
    residual,
    mod,
    mixed,
    normed,
    hidden,
    far,
    near,
    transit,
    final,
    mine,
    theirs,
    placing,
    repack,
    going,
    landed,
    turned,
    lsem,
    zsend,
    zrecv,
    rsend,
    rrecv,
    ysend,
    yrecv,
    qsend,
    qrecv,
    psend,
    precv,
    osend,
    orecv,
    wsend,
    wrecv,
    csend,
    crecv,
    asend,
    arecv,
    tsend,
    trecv,
    fsend,
    frecv,
    esend,
    erecv,
    gsend,
    grecv,
    hsend,
    hrecv,
):
    f32, bf16 = jnp.float32, jnp.bfloat16
    me = lax.axis_index("seq")
    side = lax.axis_index("cfg")
    blk = lax.axis_index("blk")
    y, z = me // Z, me % Z

    def up(t):
        return {"seq": ((y + t) % Y) * Z + z}

    def along(t):
        return {"seq": y * Z + (z + t) % Z}

    def over(t):
        return {"blk": (blk + t) % X}

    right, left, across = up(1), up(3), up(2)
    other_core = {"cfg": 1 - side}

    barrier = pltpu.get_barrier_semaphore()
    peers = [along(t) for t in range(1, Z)] + [up(t) for t in range(1, Y)]
    peers += [over(t) for t in range(1, X)] + [other_core]
    for peer in peers:
        pl.semaphore_signal(barrier, inc=1, device_id=peer, device_id_type=MESH)

    loads = [
        pltpu.make_async_copy(src, dst, lsem.at[i])
        for i, (src, dst) in enumerate(
            (
                (q_hbm.at[0], qkv.at[0]),
                (k_hbm.at[0], qkv.at[1]),
                (v_hbm.at[0], qkv.at[2]),
                (res_hbm.at[0], residual),
                (mod_hbm, mod),
                (w_out_hbm, w_out.at[0]),
                (w_up_hbm, w_up),
                (w_down_hbm, w_down),
            )
        )
    ]
    for copy in loads:
        copy.start()

    clips = clip_ref[...].astype(f32)
    first = clips[0:1, 0:1]
    count = jnp.sum(jnp.where(clips < CLIPS, 1.0, 0.0), axis=1, keepdims=True)
    row = lax.broadcasted_iota(jnp.int32, (SLOTS, SLOTS), 0).astype(f32)
    lane = lax.broadcasted_iota(jnp.int32, (SLOTS, SLOTS), 1).astype(f32)
    row_clip = jnp.where(row >= 128, 1.0, 0.0) + jnp.where(row >= 256, 1.0, 0.0)
    step = row_clip - first
    step = jnp.where(step < 0, step + 3, step)
    perm[...] = jnp.where(3 * (row - 128 * row_clip) + step == lane, 1.0, 0.0).astype(bf16)
    rank = lax.broadcasted_iota(jnp.int32, (16, 128), 1).astype(f32)
    for c in range(CLIPS):
        step = c - first
        step = jnp.where(step < 0, step + 3, step)
        bias = jnp.where(3 * rank + step < count, 0.0, NEG_FILL).astype(bf16)
        for h in range(HEADS_HERE):
            stage[3 * h + c, 384:400, :] = bias

    for which in range(3):
        loads[which].wait()
        rows = jnp.dot(perm[...], qkv[which], preferred_element_type=f32).astype(bf16)
        for h in range(HEADS_HERE):
            for c in range(CLIPS):
                stage[3 * h + c, which * 128 : which * 128 + 128, :] = rows[
                    c * 128 : c * 128 + 128, h * 128 : h * 128 + 128
                ]

    pl.semaphore_wait(barrier, len(peers))

    sends = []
    for t in NEAR_FIRST:
        copy = remote(
            stage.at[(z + t) % Z], buf.at[0, t], zsend.at[t], zrecv.at[t], along(t)
        )
        copy.start()
        sends.append(copy)
    ring = {
        1: remote(stage.at[8, KV], kv9.at[1, KV], rsend.at[1], rrecv.at[1], along(1)),
        7: remote(stage.at[8, KV], kv9.at[7, KV], rsend.at[7], rrecv.at[7], along(7)),
    }
    for copy in ring.values():
        copy.start()
    for j, peer in ((1, right), (2, left), (3, across)):
        copy = remote(stage.at[8, pl.ds(0, 128)], q9.at[j], qsend.at[j], qrecv.at[j], peer)
        copy.start()
        sends.append(copy)

    def pass_on(t):
        for j, peer in ((1, right), (2, left)):
            copy = remote(
                buf.at[0, t, KV], buf.at[j, t, KV], ysend.at[j - 1, t], yrecv.at[j - 1, t], peer
            )
            copy.start()
            sends.append(copy)

    buf[0, 0] = stage[z]
    pass_on(0)

    own_rows = pl.ds(pl.multiple_of(side * HALF, HALF), HALF)
    shares = []
    for j, t in ((1, 1), (2, 3), (3, 2)):
        copy = remote(
            w_out_hbm.at[own_rows], w_out.at[j, own_rows], wsend.at[j], wrecv.at[j], over(t)
        )
        copy.start()
        shares.append(copy)

    kv9[0] = stage[8]
    q9[0] = stage[8, 0:128, :]
    best_s[...] = jnp.full_like(best_s, NEG_FILL)
    total_s[...] = jnp.zeros_like(total_s)
    accum_s[...] = jnp.zeros_like(accum_s)

    owners = owner_ref[...].astype(f32)
    owner_column = jnp.sum(jnp.where(row == lane, owners, 0.0), axis=1, keepdims=True)
    half_start = jnp.where(lane >= HALF, float(HALF), 0.0)
    earlier = (owner_column == owners) & (row < lane) & (row >= half_start)
    ranks = jnp.sum(jnp.where(earlier, 1.0, 0.0), axis=0, keepdims=True)
    owner_y = functools.reduce(
        jnp.add, [jnp.where(owners >= edge, 1.0, 0.0) for edge in (8, 16, 24)]
    )
    target = (owners - 8 * owner_y) * 48 + owner_y * CAP + ranks
    low = side.astype(f32) * HALF
    slot = lane[0:1]
    chosen = (slot < count) & (slot >= low) & (slot < low + HALF)
    target = jnp.where(chosen, target, -1.0)
    by_slot = jnp.where(row == target, 1.0, 0.0).astype(bf16)
    half_perm = jnp.concatenate(
        [perm[pl.ds(pl.multiple_of(c * 128 + side * 64, 64), 64), :] for c in range(CLIPS)], axis=0
    )
    placing[...] = lax.dot_general(
        by_slot, half_perm, (((1,), (1,)), ((), ())), preferred_element_type=f32
    ).astype(bf16)
    from_z = jnp.floor((slot + 0.5) * (1.0 / 48.0))
    within = slot - 48 * from_z
    to_y = jnp.floor((within + 0.5) * (1.0 / CAP))
    repack[...] = jnp.where(
        row == to_y * 96 + from_z * CAP + within - CAP * to_y, 1.0, 0.0
    ).astype(bf16)

    loads[3].wait()
    for k in range(3):
        cols = slice(512 * k, 512 * k + 512)
        mixed[:, cols] = jnp.dot(perm[...], residual[:, cols], preferred_element_type=f32)

    def relay(t, onto, peer):
        ring[t].wait_recv()
        ring[onto] = remote(
            kv9.at[t, KV], kv9.at[onto, KV], rsend.at[onto], rrecv.at[onto], peer
        )
        ring[onto].start()

    for i, t in enumerate(NEAR_FIRST):
        sends[i].wait_recv()
        pass_on(t)
        if i == 1:
            relay(1, 2, along(1))
            relay(7, 6, along(7))
        if i == 3:
            relay(2, 3, along(1))
            relay(6, 5, along(7))
        if i == 5:
            relay(3, 4, along(1))
    ring[5].wait_recv()
    ring[4].wait_recv()
    for j in (1, 2, 3):
        sends[6 + j].wait_recv()

    def ninth(tile, carry):
        query = q9[pl.ds(2 * tile, 2)].reshape(256, HEAD_DIM)
        zero = jnp.zeros((256, HEAD_DIM), f32)
        best, total, accum = attend_tile(query, kv9, zero + NEG_FILL, zero, zero)
        total = jnp.sum(total, axis=1, keepdims=True)
        lane = lax.broadcasted_iota(jnp.int32, (256, HEAD_DIM), 1)
        stats = jnp.where(lane < 64, best, total)
        part_out[pl.ds(2 * tile, 2), :, 0:128] = accum.reshape(2, 128, 128)
        part_out[pl.ds(2 * tile, 2), :, 128:256] = stats.reshape(2, 128, 128)
        return carry

    lax.fori_loop(0, 2, ninth, 0)
    parts = []
    for j, onto, peer in ((1, 2, left), (2, 1, right), (3, 3, across)):
        copy = remote(part_out.at[j], part_in.at[onto], psend.at[j], precv.at[onto], peer)
        copy.start()
        parts.append(copy)

    def out_block(problem):
        row = pl.multiple_of((problem % 3) * 128, 128)
        column = pl.multiple_of((problem // 3) * 128, 128)
        return att.at[0, pl.ds(row, 128), pl.ds(column, 128)]

    def group(j, carry):
        @pl.when(j == 1)
        def _():
            for t in range(Z):
                for way, peer in ((0, right), (1, left)):
                    remote(
                        buf.at[0, t, KV], buf.at[1 + way, t, KV],
                        ysend.at[way, t], yrecv.at[way, t], peer,
                    ).wait_recv()
                    if t % 2 == way:
                        remote(
                            buf.at[1 + way, t, KV], buf.at[3, t, KV],
                            ysend.at[2, t], yrecv.at[2, t], peer,
                        ).start()

        @pl.when(j == 3)
        def _():
            for t in range(Z):
                remote(
                    buf.at[1 + t % 2, t, KV], buf.at[3, t, KV],
                    ysend.at[2, t], yrecv.at[2, t], (right, left)[t % 2],
                ).wait()

        def one(tile, inner):
            rows = pl.ds(pl.multiple_of(tile * 256, 256), 256)
            query = buf[0, pl.ds(2 * tile, 2), 0:128, :].reshape(256, HEAD_DIM)
            best, total, accum = attend_tile(
                query, buf.at[j], best_s[rows, :], total_s[rows, :], accum_s[rows, :]
            )
            best_s[rows, :] = best
            total_s[rows, :] = total
            accum_s[rows, :] = accum

            @pl.when(j == 3)
            def _():
                result = accum / jnp.sum(total, axis=1, keepdims=True)
                out_stage[pl.ds(2 * tile, 2)] = result.astype(bf16).reshape(2, 128, 128)

                @pl.when(tile == 0)
                def _():
                    pltpu.make_async_copy(out_stage.at[0], out_block(z), osend.at[0]).start()

                @pl.when(tile > 0)
                def _():
                    t = 2 * tile
                    remote(
                        out_stage.at[t], out_block(z), osend.at[t], orecv.at[t], along(Z - t)
                    ).start()

                t = 2 * tile + 1
                remote(
                    out_stage.at[t], out_block(z), osend.at[t], orecv.at[t], along(Z - t)
                ).start()

            return inner

        return lax.fori_loop(0, 4, one, carry)

    lax.fori_loop(0, 4, group, 0)

    swaps = []
    for j, copy in enumerate(shares, 1):
        copy.wait()
        swap = remote(
            w_out.at[j, own_rows], w_out.at[j, own_rows], csend.at[j], crecv.at[j], other_core
        )
        swap.start()
        swaps.append(swap)

    for copy in parts:
        copy.wait()
    pieces = [part_out.at[0], part_in.at[1], part_in.at[2], part_in.at[3]]
    bests = [piece[:, 128:129] for piece in pieces]
    top = functools.reduce(jnp.maximum, bests)
    weights = [jnp.exp2((best - top) * EXP2_SCALE) for best in bests]
    total = functools.reduce(
        jnp.add, [weight * piece[:, 192:193] for weight, piece in zip(weights, pieces)]
    )
    accum = functools.reduce(
        jnp.add, [weight * piece[:, 0:128] for weight, piece in zip(weights, pieces)]
    )
    att[0, 256:384, 256:384] = (accum / total).astype(bf16)

    pltpu.make_async_copy(out_stage.at[0], out_block(z), osend.at[0]).wait()
    for t in range(1, Z):
        remote(
            out_stage.at[t], out_block((z + t) % Z), osend.at[t], orecv.at[t], along(Z - t)
        ).wait_recv()

    gathers = {}

    def hop(src, slot, part, peer):
        rows = (TOP, LOW)[part]
        copy = remote(
            att.at[src, rows], att.at[slot, rows], asend.at[slot, part], arecv.at[slot, part], peer
        )
        copy.start()
        gathers[slot, part] = copy

    hop(0, 1, 0, over(1))
    hop(0, 2, 1, over(3))
    hop(0, 1, 1, over(1))
    hop(0, 2, 0, over(3))

    for copy in loads[4:6]:
        copy.wait()
    for copy in swaps:
        copy.wait()

    def project(slot):
        rows = att[slot]

        def one(k, carry):
            cols = pl.ds(pl.multiple_of(k * 512, 512), 512)
            term = jnp.dot(rows, w_out[slot, :, cols], preferred_element_type=f32)
            for c in range(CLIPS):
                part = slice(128 * c, 128 * c + 128)
                mixed[part, cols] += mod[c, 0:1, cols] * term[part]
            return carry

        lax.fori_loop(0, 3, one, 0)

    gathers[1, 0].wait_recv()
    hop(1, 3, 0, over(1))
    gathers[2, 1].wait_recv()
    hop(2, 3, 1, over(3))
    project(0)
    gathers[1, 1].wait_recv()
    project(1)
    gathers[2, 0].wait_recv()
    project(2)
    gathers[3, 0].wait_recv()
    gathers[3, 1].wait_recv()
    project(3)

    def normalise(k, carry):
        for c in range(CLIPS):
            rows = pl.ds(pl.multiple_of(c * 128 + k * 32, 32), 32)
            value = mixed[rows, :]
            centre = value - jnp.mean(value, axis=1, keepdims=True)
            spread = jnp.mean(centre * centre, axis=1, keepdims=True)
            scaled = centre * lax.rsqrt(spread + 1e-06) * (1.0 + mod[c, 2:3, :]) + mod[c, 1:2, :]
            normed[rows, :] = scaled.astype(bf16)
        return carry

    lax.fori_loop(0, 4, normalise, 0)

    loads[6].wait()

    def expand(k, carry):
        cols = pl.ds(pl.multiple_of(k * 512, 512), 512)
        value = jnp.dot(normed[...], w_up[:, cols], preferred_element_type=f32)
        hidden[:, cols] = jax.nn.gelu(value, approximate=True).astype(bf16)
        return carry

    lax.fori_loop(0, 3, expand, 0)

    loads[7].wait()

    def contract(t):
        cols = pl.ds(pl.multiple_of(((blk + t) % X) * SLOTS, SLOTS), SLOTS)
        return jnp.dot(hidden[...], w_down[:, cols], preferred_element_type=f32)

    far[...] = contract(2).astype(bf16)
    passing = [
        remote(far.at[TOP], transit.at[0], tsend.at[0], trecv.at[0], over(1)),
        remote(far.at[LOW], transit.at[1], tsend.at[1], trecv.at[1], over(3)),
    ]
    for copy in passing:
        copy.start()
    finals = [
        remote(near.at[0, TOP], final.at[0], fsend.at[0], frecv.at[0], over(1)),
        remote(near.at[0, LOW], final.at[1], fsend.at[1], frecv.at[1], over(1)),
        remote(near.at[1, TOP], final.at[2], fsend.at[2], frecv.at[2], over(3)),
        remote(near.at[1, LOW], final.at[3], fsend.at[3], frecv.at[3], over(3)),
    ]
    to_right = contract(1)
    near[0, HALF:] = to_right[HALF:].astype(bf16)
    finals[1].start()
    to_left = contract(3)
    near[1, :HALF] = to_left[:HALF].astype(bf16)
    finals[2].start()
    passing[0].wait_recv()
    near[0, :HALF] = (to_right[:HALF] + transit[0].astype(f32)).astype(bf16)
    finals[0].start()
    passing[1].wait_recv()
    near[1, HALF:] = (to_left[HALF:] + transit[1].astype(f32)).astype(bf16)
    finals[3].start()
    own = contract(0)
    for copy in finals:
        copy.wait_recv()
    own_cols = pl.ds(pl.multiple_of(blk * SLOTS, SLOTS), SLOTS)
    for c in range(CLIPS):
        for half in range(2):
            start = c * 128 + half * 64
            which, rows = start // HALF, slice(start % HALF, start % HALF + 64)
            summed = own[start : start + 64] + final[which, rows].astype(f32)
            summed = summed + final[2 + which, rows].astype(f32)
            value = mixed[start : start + 64, own_cols] + mod[c, 3:4, own_cols] * summed
            mine[half, c * 64 : c * 64 + 64] = value.astype(bf16)

    exchange = remote(mine.at[1 - side], theirs, esend.at[0], erecv.at[0], other_core)
    exchange.start()
    exchange.wait_recv()
    ours, others = mine[side].astype(f32), theirs[...].astype(f32)
    conditional = jnp.where(side == 0, ours, others)
    plain = jnp.where(side == 0, others, ours)
    guided = jnp.concatenate(
        [
            plain[64 * c : 64 * c + 64]
            + guide_ref[c] * (conditional[64 * c : 64 * c + 64] - plain[64 * c : 64 * c + 64])
            for c in range(CLIPS)
        ],
        axis=0,
    ).astype(bf16)

    here = pl.ds(pl.multiple_of(z * 48, 16), 48)
    trips, last = [], []
    for k in range(3):
        going[k] = jnp.dot(
            placing[...], guided[:, 128 * k : 128 * k + 128], preferred_element_type=f32
        ).astype(bf16)
        for t in NEAR_FIRST:
            there = pl.ds(pl.multiple_of(((z + t) % Z) * 48, 16), 48)
            copy = remote(
                going.at[k, there], landed.at[k, here], gsend.at[k, t], grecv.at[k, t], along(t)
            )
            copy.start()
            trips.append(copy)
        landed[k, here, :] = going[k, here, :]
    row_here = pl.ds(pl.multiple_of(y * 96, 96), 96)
    for k in range(3):
        cols = pl.ds(128 * k, 128)
        for copy in trips[7 * k : 7 * k + 7]:
            copy.wait_recv()
        turned[k] = jnp.dot(repack[...], landed[k], preferred_element_type=f32).astype(bf16)
        for t in (1, 3, 2):
            there = pl.ds(pl.multiple_of(((y + t) % Y) * 96, 96), 96)
            copy = remote(
                turned.at[k, there], out_ref.at[0, row_here, cols],
                hsend.at[k, t], hrecv.at[k, t], up(t),
            )
            copy.start()
            last.append(copy)
        out_ref[0, row_here, 128 * k : 128 * k + 128] = turned[k, row_here, :]
    for copy in last:
        copy.wait()

    for t in range(1, Z):
        remote(
            out_stage.at[t], out_block((z + t) % Z), osend.at[t], orecv.at[t], along(Z - t)
        ).wait_send()
    for copy in [*sends, *ring.values(), *gathers.values(), *passing, *finals, exchange, *trips]:
        copy.wait_send()


def block(clips, owners, guide_scale, *arrays):
    dma = pltpu.SemaphoreType.DMA
    vmem = pltpu.VMEM
    f32, bf16 = jnp.float32, jnp.bfloat16
    return pl.pallas_call(
        block_kernel,
        out_shape=jax.ShapeDtypeStruct((1, SLOTS, SLOTS), bf16),
        in_specs=[
            pl.BlockSpec(memory_space=vmem),
            pl.BlockSpec(memory_space=vmem),
            pl.BlockSpec(memory_space=pltpu.SMEM),
            *[pl.BlockSpec(memory_space=pl.ANY)] * 8,
        ],
        out_specs=pl.BlockSpec(memory_space=vmem),
        scratch_shapes=[
            vmem((3, SLOTS, SLOTS), bf16),
            vmem((SLOTS, SLOTS), bf16),
            vmem((9, MSG, 128), bf16),
            vmem((4, Z, MSG, 128), bf16),
            vmem((Z, MSG, 128), bf16),
            vmem((4, 128, 128), bf16),
            vmem((4, 128, 256), f32),
            vmem((4, 128, 256), f32),
            vmem((1024, 128), f32),
            vmem((1024, 128), f32),
            vmem((1024, 128), f32),
            vmem((Z, 128, 128), bf16),
            vmem((4, SLOTS, SLOTS), bf16),
            vmem((4, SLOTS, D), bf16),
            vmem((D, D), bf16),
            vmem((D, D), bf16),
            vmem((SLOTS, D), bf16),
            vmem((CLIPS, 4, D), f32),
            vmem((SLOTS, D), f32),
            vmem((SLOTS, D), bf16),
            vmem((SLOTS, D), bf16),
            vmem((SLOTS, SLOTS), bf16),
            vmem((2, SLOTS, SLOTS), bf16),
            vmem((2, HALF, SLOTS), bf16),
            vmem((4, HALF, SLOTS), bf16),
            vmem((2, HALF, SLOTS), bf16),
            vmem((HALF, SLOTS), bf16),
            vmem((SLOTS, HALF), bf16),
            vmem((SLOTS, SLOTS), bf16),
            vmem((3, SLOTS, 128), bf16),
            vmem((3, SLOTS, 128), bf16),
            vmem((3, SLOTS, 128), bf16),
            dma((8,)),
            dma((Z,)),
            dma((Z,)),
            dma((Z,)),
            dma((Z,)),
            dma((3, Z)),
            dma((3, Z)),
            dma((4,)),
            dma((4,)),
            dma((4,)),
            dma((4,)),
            dma((Z,)),
            dma((Z,)),
            dma((4,)),
            dma((4,)),
            dma((4,)),
            dma((4,)),
            dma((4, 2)),
            dma((4, 2)),
            dma((2,)),
            dma((2,)),
            dma((4,)),
            dma((4,)),
            dma((1,)),
            dma((1,)),
            dma((3, Z)),
            dma((3, Z)),
            dma((3, Y)),
            dma((3, Y)),
        ],
        compiler_params=pltpu.CompilerParams(
            collective_id=0, has_side_effects=True, vmem_limit_bytes=56 * 2**20
        ),
        name="guided_block",
    )(clips, owners, guide_scale, *arrays)


def shards(
    queries, keys, values, residual, w_out, w_up, w_down, modulation, guide_scale, slot_clip, owner
):
    return block(
        slot_clip.reshape(1, SLOTS),
        owner.reshape(1, SLOTS),
        guide_scale,
        queries,
        keys,
        values,
        residual,
        modulation,
        w_out,
        w_up,
        w_down,
    )


def solution(mesh):
    placed = (
        P("cfg", "seq", "blk"),
        P("cfg", "seq", "blk"),
        P("cfg", "seq", "blk"),
        P("cfg", "seq", None),
        P("blk", None),
        P(None, "blk"),
        P("blk", None),
        P(),
        P(),
        P("seq"),
        P("seq", None),
    )
    return jax.shard_map(
        shards, mesh=mesh, in_specs=placed, out_specs=P("cfg", "seq", "blk"), check_vma=False
    )
```

time: 213 us -> 109 us (0.51)
  waiting for transfers between devices: 72.3 us -> 0 us
  Pallas kernels: 60.7 us -> 104 us
  blocking collectives: 25.2 us -> 0 us
  local copies, waits for them, and re-layouts: 18.2 us -> 2.95 us
  matrix products: 14.3 us -> 0 us
  between operations: 13.6 us -> 0.01 us
  other arithmetic: 7.76 us -> 0 us
    psum x1 -> x0, waiting for transfers between devices: 48.3 us -> none  [shards(): lax.psum(partial_out.astype(jnp.bfloat16), 'blk').astype(jnp.float32)]
    pallas_call x1, Pallas kernels: 60.7 us -> 104 us  [block(): pl.pallas_call(block_kernel, out_shape=jax.ShapeDtypeStruct((1, SLOTS, SL...]
    all_to_all x1 -> x0, blocking collectives: 25.2 us -> none  [shards(): lax.all_to_all(outgoing, 'seq', split_axis=0, concat_axis=0, tiled=True)]
    unnamed x3 -> x0, waiting for transfers between devices: 23.5 us -> none
    dot_general x4 -> x0, matrix products: 14.3 us -> none  [the longest x1 10 us: shards(): terms = jnp.dot(hidden, w_down, preferred_element_type=jnp.float32)]
    unnamed x23 -> x1, local copies, waits for them, and re-layouts: 11.5 us -> 1.71 us
    slice x2 -> x0, local copies, waits for them, and re-layouts: 4.51 us -> none  [the longest x1 3.22 us: shards(): gate_mlp = lax.dynamic_slice_in_dim(mod[:, 3], col_start, columns, 1)]
    convert_element_type x4 -> x0, other arithmetic: 3.68 us -> none  [the longest x1 1.28 us: shards(): jnp.where(live, 0.0, NEG_FILL).astype(jnp.bfloat16).reshape(CLIPS, 1, GROUP)]
  transfers between devices with their start and end apart: 3 -> 0, of which waited for: 3 -> 0; matrix products, arithmetic and copies ran while one was open for 2% -> 0% of each run, Pallas kernels for 0% -> 0%
where the time goes in v2:
time: 109 us; the launch traced here: 107 us
  Pallas kernels  104 us (95%)
  local copies, waits for them, and re-layouts  2.95 us (3%)
    pallas_call x1, Pallas kernels, block(): pl.pallas_call(block_kernel, out_shape=jax.ShapeDtypeStruct((1, SLOTS, SL...  104 us

profile of v2, /device:TPU:32, one launch (start us, length us, event | category | flops | bytes accessed | tf_op | source)
XLA Modules:
  0.0 107.3 jit_solution(17028682742429817612)
XLA Ops:
  0.0 1.2 %reshape.6.clip_ref = s32[1,384]{1,0:T(1,128)} reshape(s32[384]{0:T(512)} %param.20) | data formatting | bytes 3072 | tf_op jit(solution)/shard_map/reshape | solution.py:672
  1.2 104.4 %guided_block.1 = bf16[1,384,384]{2,1,0:T(8,128)(2,1)} custom-call(s32[1,384]{1,0:T(1,128)} %reshape.6.clip_ref, s32[1,384]{1,0:T(1,128)} %bitcast.1, f32[3]{0:T(128)} %guide_ref.1, bf16[1,384,384]{2,1,0:T(8,128)(2,1)} %q_hbm.1, bf16[1,384,384]{2,1,0:T(8,128)(2,1)} %k_hbm.1, bf16[1,384,384]{2,1,0:T(8,128)(2,1)} %v_hbm.1, bf16[1,384,1536]{2,1,0:T(8,128)(2,1)} %res_hbm.1, ...), custom_call_target="tpu_custom_call" | custom-call | tf_op jit(solution)/shard_map/guided_block/pallas_call | solution.py:588
  105.6 1.7 %copy.13 = bf16[1,384,384]{2,1,0:T(8,128)(2,1)} copy(bf16[1,384,384]{2,1,0:T(8,128)(2,1)} %guided_block.1) | data formatting | bytes 589824

commit v3 on v2

--- a/solution.py
+++ b/solution.py
@@ -39,12 +39,13 @@
 
 
 def attend_tile(query, kv, best, total, accum):
-    keys = kv[:, 128:256, :].reshape(8 * GROUP, HEAD_DIM)
+    count = kv.shape[0]
+    keys = kv[:, 128:256, :].reshape(count * GROUP, HEAD_DIM)
     scores = lax.dot_general(
         query, keys, (((1,), (1,)), ((), ())), preferred_element_type=jnp.float32
     )
     pieces = []
-    for i in range(8):
+    for i in range(count):
         bias = kv[i, 384:400, :].astype(jnp.float32)[0:1]
         pieces.append(scores[:, i * GROUP : (i + 1) * GROUP] + bias)
     peak = functools.reduce(jnp.maximum, pieces)
@@ -53,7 +54,7 @@
     fade = jnp.exp2((best - new_best) * EXP2_SCALE)
     total = total * fade + functools.reduce(jnp.add, probs)
     weights = jnp.concatenate([prob.astype(jnp.bfloat16) for prob in probs], axis=1)
-    values = kv[:, 256:384, :].reshape(8 * GROUP, HEAD_DIM)
+    values = kv[:, 256:384, :].reshape(count * GROUP, HEAD_DIM)
     accum = accum * fade + jnp.dot(weights, values, preferred_element_type=jnp.float32)
     return new_best, total, accum
 
@@ -79,6 +80,8 @@
     q9,
     part_out,
     part_in,
+    stat_out,
+    stat_in,
     best_s,
     total_s,
     accum_s,
@@ -94,6 +97,7 @@
     hidden,
     far,
     near,
+    ready,
     transit,
     final,
     mine,
@@ -114,6 +118,8 @@
     qrecv,
     psend,
     precv,
+    ssend,
+    srecv,
     osend,
     orecv,
     wsend,
@@ -203,19 +209,19 @@
 
     pl.semaphore_wait(barrier, len(peers))
 
-    sends = []
-    for t in NEAR_FIRST:
-        copy = remote(
-            stage.at[(z + t) % Z], buf.at[0, t], zsend.at[t], zrecv.at[t], along(t)
-        )
-        copy.start()
-        sends.append(copy)
     ring = {
         1: remote(stage.at[8, KV], kv9.at[1, KV], rsend.at[1], rrecv.at[1], along(1)),
         7: remote(stage.at[8, KV], kv9.at[7, KV], rsend.at[7], rrecv.at[7], along(7)),
     }
     for copy in ring.values():
         copy.start()
+    sends = []
+    for t in NEAR_FIRST:
+        copy = remote(
+            stage.at[(z + t) % Z], buf.at[0, t], zsend.at[t], zrecv.at[t], along(t)
+        )
+        copy.start()
+        sends.append(copy)
     for j, peer in ((1, right), (2, left), (3, across)):
         copy = remote(stage.at[8, pl.ds(0, 128)], q9.at[j], qsend.at[j], qrecv.at[j], peer)
         copy.start()
@@ -246,6 +252,13 @@
     best_s[...] = jnp.full_like(best_s, NEG_FILL)
     total_s[...] = jnp.zeros_like(total_s)
     accum_s[...] = jnp.zeros_like(accum_s)
+
+    def relay(t, onto, peer):
+        ring[t].wait_recv()
+        ring[onto] = remote(
+            kv9.at[t, KV], kv9.at[onto, KV], rsend.at[onto], rrecv.at[onto], peer
+        )
+        ring[onto].start()
 
     owners = owner_ref[...].astype(f32)
     owner_column = jnp.sum(jnp.where(row == lane, owners, 0.0), axis=1, keepdims=True)
@@ -279,12 +292,45 @@
         cols = slice(512 * k, 512 * k + 512)
         mixed[:, cols] = jnp.dot(perm[...], residual[:, cols], preferred_element_type=f32)
 
-    def relay(t, onto, peer):
-        ring[t].wait_recv()
-        ring[onto] = remote(
-            kv9.at[t, KV], kv9.at[onto, KV], rsend.at[onto], rrecv.at[onto], peer
-        )
-        ring[onto].start()
+    def out_block(problem):
+        row = pl.multiple_of((problem % 3) * 128, 128)
+        column = pl.multiple_of((problem // 3) * 128, 128)
+        return att.at[0, pl.ds(row, 128), pl.ds(column, 128)]
+
+    def returning(t):
+        return remote(
+            out_stage.at[t], out_block(z), osend.at[t], orecv.at[t], along((Z - t) % Z)
+        )
+
+    def from_row(way, t):
+        return remote(
+            buf.at[0, t, KV], buf.at[1 + way, t, KV],
+            ysend.at[way, t], yrecv.at[way, t], (right, left)[way],
+        )
+
+    def far_row(t):
+        return remote(
+            buf.at[1 + t % 2, t, KV], buf.at[3, t, KV],
+            ysend.at[2, t], yrecv.at[2, t], (right, left)[t % 2],
+        )
+
+    def attend(j, tile):
+        rows = pl.ds(pl.multiple_of(tile * 256, 256), 256)
+        query = buf[0, pl.ds(2 * tile, 2), 0:128, :].reshape(256, HEAD_DIM)
+        best, total, accum = attend_tile(
+            query, buf.at[j], best_s[rows, :], total_s[rows, :], accum_s[rows, :]
+        )
+        best_s[rows, :] = best
+        total_s[rows, :] = total
+        accum_s[rows, :] = accum
+        return total, accum
+
+    def group(j):
+        def one(tile, carry):
+            attend(j, tile)
+            return carry
+
+        lax.fori_loop(0, 4, one, 0)
 
     for i, t in enumerate(NEAR_FIRST):
         sends[i].wait_recv()
@@ -292,98 +338,66 @@
         if i == 1:
             relay(1, 2, along(1))
             relay(7, 6, along(7))
-        if i == 3:
-            relay(2, 3, along(1))
-            relay(6, 5, along(7))
-        if i == 5:
-            relay(3, 4, along(1))
+    relay(2, 3, along(1))
+    relay(6, 5, along(7))
+    group(0)
+    relay(3, 4, along(1))
+    for t in range(Z):
+        for way in (0, 1):
+            from_row(way, t).wait_recv()
+        far_row(t).start()
+    group(1)
+    group(2)
+
     ring[5].wait_recv()
     ring[4].wait_recv()
     for j in (1, 2, 3):
         sends[6 + j].wait_recv()
+    corner = lax.broadcasted_iota(jnp.int32, (128, 128), 0) == lax.broadcasted_iota(
+        jnp.int32, (128, 128), 1
+    )
 
     def ninth(tile, carry):
         query = q9[pl.ds(2 * tile, 2)].reshape(256, HEAD_DIM)
         zero = jnp.zeros((256, HEAD_DIM), f32)
         best, total, accum = attend_tile(query, kv9, zero + NEG_FILL, zero, zero)
         total = jnp.sum(total, axis=1, keepdims=True)
-        lane = lax.broadcasted_iota(jnp.int32, (256, HEAD_DIM), 1)
-        stats = jnp.where(lane < 64, best, total)
-        part_out[pl.ds(2 * tile, 2), :, 0:128] = accum.reshape(2, 128, 128)
-        part_out[pl.ds(2 * tile, 2), :, 128:256] = stats.reshape(2, 128, 128)
+        part_out[pl.ds(2 * tile, 2)] = (accum / total).astype(bf16).reshape(2, 128, 128)
+        for i in range(2):
+            rows = slice(128 * i, 128 * i + 128)
+            for at, column in ((0, best[rows, 0:1]), (8, total[rows])):
+                line = jnp.sum(jnp.where(corner, column, 0.0), axis=0, keepdims=True)
+                stat_out[2 * tile + i, at : at + 8, :] = jnp.broadcast_to(line, (8, 128))
         return carry
 
     lax.fori_loop(0, 2, ninth, 0)
     parts = []
     for j, onto, peer in ((1, 2, left), (2, 1, right), (3, 3, across)):
-        copy = remote(part_out.at[j], part_in.at[onto], psend.at[j], precv.at[onto], peer)
-        copy.start()
-        parts.append(copy)
-
-    def out_block(problem):
-        row = pl.multiple_of((problem % 3) * 128, 128)
-        column = pl.multiple_of((problem // 3) * 128, 128)
-        return att.at[0, pl.ds(row, 128), pl.ds(column, 128)]
-
-    def group(j, carry):
-        @pl.when(j == 1)
+        for copy in (
+            remote(part_out.at[j], part_in.at[onto], psend.at[j], precv.at[onto], peer),
+            remote(stat_out.at[j], stat_in.at[onto], ssend.at[j], srecv.at[onto], peer),
+        ):
+            copy.start()
+            parts.append(copy)
+
+    for t in range(Z):
+        far_row(t).wait()
+
+    def finish_tile(tile, carry):
+        total, accum = attend(3, tile)
+        result = accum / jnp.sum(total, axis=1, keepdims=True)
+        out_stage[pl.ds(2 * tile, 2)] = result.astype(bf16).reshape(2, 128, 128)
+
+        @pl.when(tile > 0)
         def _():
-            for t in range(Z):
-                for way, peer in ((0, right), (1, left)):
-                    remote(
-                        buf.at[0, t, KV], buf.at[1 + way, t, KV],
-                        ysend.at[way, t], yrecv.at[way, t], peer,
-                    ).wait_recv()
-                    if t % 2 == way:
-                        remote(
-                            buf.at[1 + way, t, KV], buf.at[3, t, KV],
-                            ysend.at[2, t], yrecv.at[2, t], peer,
-                        ).start()
-
-        @pl.when(j == 3)
-        def _():
-            for t in range(Z):
-                remote(
-                    buf.at[1 + t % 2, t, KV], buf.at[3, t, KV],
-                    ysend.at[2, t], yrecv.at[2, t], (right, left)[t % 2],
-                ).wait()
-
-        def one(tile, inner):
-            rows = pl.ds(pl.multiple_of(tile * 256, 256), 256)
-            query = buf[0, pl.ds(2 * tile, 2), 0:128, :].reshape(256, HEAD_DIM)
-            best, total, accum = attend_tile(
-                query, buf.at[j], best_s[rows, :], total_s[rows, :], accum_s[rows, :]
-            )
-            best_s[rows, :] = best
-            total_s[rows, :] = total
-            accum_s[rows, :] = accum
-
-            @pl.when(j == 3)
-            def _():
-                result = accum / jnp.sum(total, axis=1, keepdims=True)
-                out_stage[pl.ds(2 * tile, 2)] = result.astype(bf16).reshape(2, 128, 128)
-
-                @pl.when(tile == 0)
-                def _():
-                    pltpu.make_async_copy(out_stage.at[0], out_block(z), osend.at[0]).start()
-
-                @pl.when(tile > 0)
-                def _():
-                    t = 2 * tile
-                    remote(
-                        out_stage.at[t], out_block(z), osend.at[t], orecv.at[t], along(Z - t)
-                    ).start()
-
-                t = 2 * tile + 1
-                remote(
-                    out_stage.at[t], out_block(z), osend.at[t], orecv.at[t], along(Z - t)
-                ).start()
-
-            return inner
-
-        return lax.fori_loop(0, 4, one, carry)
-
-    lax.fori_loop(0, 4, group, 0)
+            returning(2 * tile).start()
+
+        returning(2 * tile + 1).start()
+        return carry
+
+    lax.fori_loop(0, 4, finish_tile, 0)
+    own_block = pltpu.make_async_copy(out_stage.at[0], out_block(z), osend.at[0])
+    own_block.start()
 
     swaps = []
     for j, copy in enumerate(shares, 1):
@@ -396,19 +410,25 @@
 
     for copy in parts:
         copy.wait()
+    lines = [stat_out.at[0], stat_in.at[1], stat_in.at[2], stat_in.at[3]]
     pieces = [part_out.at[0], part_in.at[1], part_in.at[2], part_in.at[3]]
-    bests = [piece[:, 128:129] for piece in pieces]
+    bests = [line[0:1, :] for line in lines]
     top = functools.reduce(jnp.maximum, bests)
-    weights = [jnp.exp2((best - top) * EXP2_SCALE) for best in bests]
-    total = functools.reduce(
-        jnp.add, [weight * piece[:, 192:193] for weight, piece in zip(weights, pieces)]
-    )
+    weights = [
+        jnp.exp2((best - top) * EXP2_SCALE) * line[8:9, :] for best, line in zip(bests, lines)
+    ]
+    total = functools.reduce(jnp.add, weights)
     accum = functools.reduce(
-        jnp.add, [weight * piece[:, 0:128] for weight, piece in zip(weights, pieces)]
-    )
-    att[0, 256:384, 256:384] = (accum / total).astype(bf16)
-
-    pltpu.make_async_copy(out_stage.at[0], out_block(z), osend.at[0]).wait()
+        jnp.add,
+        [
+            jnp.sum(jnp.where(corner, weight / total, 0.0), axis=1, keepdims=True)
+            * piece[...].astype(f32)
+            for weight, piece in zip(weights, pieces)
+        ],
+    )
+    att[0, 256:384, 256:384] = accum.astype(bf16)
+
+    own_block.wait()
     for t in range(1, Z):
         remote(
             out_stage.at[t], out_block((z + t) % Z), osend.at[t], orecv.at[t], along(Z - t)
@@ -488,65 +508,78 @@
         cols = pl.ds(pl.multiple_of(((blk + t) % X) * SLOTS, SLOTS), SLOTS)
         return jnp.dot(hidden[...], w_down[:, cols], preferred_element_type=f32)
 
-    far[...] = contract(2).astype(bf16)
-    passing = [
-        remote(far.at[TOP], transit.at[0], tsend.at[0], trecv.at[0], over(1)),
-        remote(far.at[LOW], transit.at[1], tsend.at[1], trecv.at[1], over(3)),
-    ]
-    for copy in passing:
-        copy.start()
-    finals = [
-        remote(near.at[0, TOP], final.at[0], fsend.at[0], frecv.at[0], over(1)),
-        remote(near.at[0, LOW], final.at[1], fsend.at[1], frecv.at[1], over(1)),
-        remote(near.at[1, TOP], final.at[2], fsend.at[2], frecv.at[2], over(3)),
-        remote(near.at[1, LOW], final.at[3], fsend.at[3], frecv.at[3], over(3)),
-    ]
-    to_right = contract(1)
-    near[0, HALF:] = to_right[HALF:].astype(bf16)
-    finals[1].start()
-    to_left = contract(3)
-    near[1, :HALF] = to_left[:HALF].astype(bf16)
-    finals[2].start()
-    passing[0].wait_recv()
-    near[0, :HALF] = (to_right[:HALF] + transit[0].astype(f32)).astype(bf16)
-    finals[0].start()
-    passing[1].wait_recv()
-    near[1, HALF:] = (to_left[HALF:] + transit[1].astype(f32)).astype(bf16)
-    finals[3].start()
-    own = contract(0)
-    for copy in finals:
-        copy.wait_recv()
-    own_cols = pl.ds(pl.multiple_of(blk * SLOTS, SLOTS), SLOTS)
-    for c in range(CLIPS):
-        for half in range(2):
-            start = c * 128 + half * 64
-            which, rows = start // HALF, slice(start % HALF, start % HALF + 64)
-            summed = own[start : start + 64] + final[which, rows].astype(f32)
-            summed = summed + final[2 + which, rows].astype(f32)
-            value = mixed[start : start + 64, own_cols] + mod[c, 3:4, own_cols] * summed
-            mine[half, c * 64 : c * 64 + 64] = value.astype(bf16)
-
-    exchange = remote(mine.at[1 - side], theirs, esend.at[0], erecv.at[0], other_core)
-    exchange.start()
-    exchange.wait_recv()
-    ours, others = mine[side].astype(f32), theirs[...].astype(f32)
-    conditional = jnp.where(side == 0, ours, others)
-    plain = jnp.where(side == 0, others, ours)
-    guided = jnp.concatenate(
-        [
-            plain[64 * c : 64 * c + 64]
-            + guide_ref[c] * (conditional[64 * c : 64 * c + 64] - plain[64 * c : 64 * c + 64])
-            for c in range(CLIPS)
-        ],
-        axis=0,
-    ).astype(bf16)
+    passing, finals = {}, {}
+
+    def chunk(k):
+        return slice(128 * k, 128 * k + 128)
+
+    def give_far():
+        far_terms = contract(2).astype(bf16)
+        for k in range(3):
+            far[k] = far_terms[:, chunk(k)]
+            for way, rows in ((0, TOP), (1, LOW)):
+                passing[way, k] = remote(
+                    far.at[k, rows], transit.at[way, k],
+                    tsend.at[way, k], trecv.at[way, k], over((1, 3)[way]),
+                )
+                passing[way, k].start()
+
+    def give_near(way):
+        terms = contract((1, 3)[way])
+        low = (HALF, 0)[way]
+        for k in range(3):
+            near[way, k] = terms[:, chunk(k)]
+            ready[1 + way, k] = terms[low : low + HALF, chunk(k)].astype(bf16)
+            deliver(1 + way, k)
+
+    def deliver(which, k):
+        finals[which, k] = remote(
+            ready.at[which, k], final.at[which, k],
+            fsend.at[which, k], frecv.at[which, k], over((1, 1, 3, 3)[which]),
+        )
+        finals[which, k].start()
+
+    def merge(k):
+        for way, which, rows in ((0, 0, TOP), (1, 3, LOW)):
+            passing[way, k].wait_recv()
+            ready[which, k] = (near[way, k, rows, :] + transit[way, k].astype(f32)).astype(bf16)
+            deliver(which, k)
+
+    exchanges, trips, last = {}, [], []
+
+    def finish(k):
+        for which in range(4):
+            finals[which, k].wait_recv()
+        cols = pl.ds(pl.multiple_of(blk * SLOTS + 128 * k, 128), 128)
+        for c in range(CLIPS):
+            for half in range(2):
+                start = c * 128 + half * 64
+                which, rows = start // HALF, slice(start % HALF, start % HALF + 64)
+                summed = own[start : start + 64, chunk(k)] + final[which, k, rows].astype(f32)
+                summed = summed + final[2 + which, k, rows].astype(f32)
+                value = mixed[start : start + 64, cols] + mod[c, 3:4, cols] * summed
+                mine[half, k, c * 64 : c * 64 + 64] = value.astype(bf16)
+        exchanges[k] = remote(
+            mine.at[1 - side, k], theirs.at[k], esend.at[k], erecv.at[k], other_core
+        )
+        exchanges[k].start()
 
     here = pl.ds(pl.multiple_of(z * 48, 16), 48)
-    trips, last = [], []
-    for k in range(3):
-        going[k] = jnp.dot(
-            placing[...], guided[:, 128 * k : 128 * k + 128], preferred_element_type=f32
+
+    def send_rows(k):
+        exchanges[k].wait_recv()
+        ours, others = mine[side, k].astype(f32), theirs[k].astype(f32)
+        conditional = jnp.where(side == 0, ours, others)
+        plain = jnp.where(side == 0, others, ours)
+        guided = jnp.concatenate(
+            [
+                plain[64 * c : 64 * c + 64]
+                + guide_ref[c] * (conditional[64 * c : 64 * c + 64] - plain[64 * c : 64 * c + 64])
+                for c in range(CLIPS)
+            ],
+            axis=0,
         ).astype(bf16)
+        going[k] = jnp.dot(placing[...], guided, preferred_element_type=f32).astype(bf16)
         for t in NEAR_FIRST:
             there = pl.ds(pl.multiple_of(((z + t) % Z) * 48, 16), 48)
             copy = remote(
@@ -555,8 +588,10 @@
             copy.start()
             trips.append(copy)
         landed[k, here, :] = going[k, here, :]
+
     row_here = pl.ds(pl.multiple_of(y * 96, 96), 96)
-    for k in range(3):
+
+    def turn_rows(k):
         cols = pl.ds(128 * k, 128)
         for copy in trips[7 * k : 7 * k + 7]:
             copy.wait_recv()
@@ -570,14 +605,32 @@
             copy.start()
             last.append(copy)
         out_ref[0, row_here, 128 * k : 128 * k + 128] = turned[k, row_here, :]
+
+    give_far()
+    give_near(0)
+    give_near(1)
+    merge(0)
+    merge(1)
+    merge(2)
+    own = contract(0)
+    finish(0)
+    finish(1)
+    send_rows(0)
+    finish(2)
+    send_rows(1)
+    turn_rows(0)
+    send_rows(2)
+    turn_rows(1)
+    turn_rows(2)
     for copy in last:
         copy.wait()
 
     for t in range(1, Z):
-        remote(
-            out_stage.at[t], out_block((z + t) % Z), osend.at[t], orecv.at[t], along(Z - t)
-        ).wait_send()
-    for copy in [*sends, *ring.values(), *gathers.values(), *passing, *finals, exchange, *trips]:
+        returning(t).wait_send()
+    for copy in [
+        *sends, *ring.values(), *gathers.values(), *passing.values(), *finals.values(),
+        *exchanges.values(), *trips,
+    ]:
         copy.wait_send()
 
 
@@ -602,8 +655,10 @@
             vmem((4, Z, MSG, 128), bf16),
             vmem((Z, MSG, 128), bf16),
             vmem((4, 128, 128), bf16),
-            vmem((4, 128, 256), f32),
-            vmem((4, 128, 256), f32),
+            vmem((4, 128, 128), bf16),
+            vmem((4, 128, 128), bf16),
+            vmem((4, 16, 128), f32),
+            vmem((4, 16, 128), f32),
             vmem((1024, 128), f32),
             vmem((1024, 128), f32),
             vmem((1024, 128), f32),
@@ -617,46 +672,30 @@
             vmem((SLOTS, D), f32),
             vmem((SLOTS, D), bf16),
             vmem((SLOTS, D), bf16),
-            vmem((SLOTS, SLOTS), bf16),
-            vmem((2, SLOTS, SLOTS), bf16),
-            vmem((2, HALF, SLOTS), bf16),
-            vmem((4, HALF, SLOTS), bf16),
-            vmem((2, HALF, SLOTS), bf16),
-            vmem((HALF, SLOTS), bf16),
+            vmem((3, SLOTS, 128), bf16),
+            vmem((2, 3, SLOTS, 128), f32),
+            vmem((4, 3, HALF, 128), bf16),
+            vmem((2, 3, HALF, 128), bf16),
+            vmem((4, 3, HALF, 128), bf16),
+            vmem((2, 3, HALF, 128), bf16),
+            vmem((3, HALF, 128), bf16),
             vmem((SLOTS, HALF), bf16),
             vmem((SLOTS, SLOTS), bf16),
             vmem((3, SLOTS, 128), bf16),
             vmem((3, SLOTS, 128), bf16),
             vmem((3, SLOTS, 128), bf16),
             dma((8,)),
-            dma((Z,)),
-            dma((Z,)),
-            dma((Z,)),
-            dma((Z,)),
-            dma((3, Z)),
-            dma((3, Z)),
-            dma((4,)),
-            dma((4,)),
-            dma((4,)),
-            dma((4,)),
-            dma((Z,)),
-            dma((Z,)),
-            dma((4,)),
-            dma((4,)),
-            dma((4,)),
-            dma((4,)),
-            dma((4, 2)),
-            dma((4, 2)),
-            dma((2,)),
-            dma((2,)),
-            dma((4,)),
-            dma((4,)),
-            dma((1,)),
-            dma((1,)),
-            dma((3, Z)),
-            dma((3, Z)),
-            dma((3, Y)),
-            dma((3, Y)),
+            *[dma((Z,))] * 4,
+            *[dma((3, Z))] * 2,
+            *[dma((4,))] * 6,
+            *[dma((Z,))] * 2,
+            *[dma((4,))] * 4,
+            *[dma((4, 2))] * 2,
+            *[dma((2, 3))] * 2,
+            *[dma((4, 3))] * 2,
+            *[dma((3,))] * 2,
+            *[dma((3, Z))] * 2,
+            *[dma((3, Y))] * 2,
         ],
         compiler_params=pltpu.CompilerParams(
             collective_id=0, has_side_effects=True, vmem_limit_bytes=56 * 2**20

time: 109 us -> 98.1 us (0.90); the launches traced: 107 us -> 98 us
  Pallas kernels: 104 us -> 95 us
    pallas_call x1, Pallas kernels: 104 us -> 95 us  [block(): pl.pallas_call(block_kernel, out_shape=jax.ShapeDtypeStruct((1, SLOTS, SL...]
where the time goes in v3:
time: 98.1 us; the launch traced here: 98 us
  Pallas kernels  95 us (97%)
  local copies, waits for them, and re-layouts  2.95 us (3%)
    pallas_call x1, Pallas kernels, block(): pl.pallas_call(block_kernel, out_shape=jax.ShapeDtypeStruct((1, SLOTS, SL...  95 us

profile of v3, /device:TPU:32, one launch (start us, length us, event | category | flops | bytes accessed | tf_op | source)
XLA Modules:
  0.0 98.0 jit_solution(10708200365096431464)
XLA Ops:
  0.0 1.2 %reshape.6.clip_ref = s32[1,384]{1,0:T(1,128)} reshape(s32[384]{0:T(512)} %param.20) | data formatting | bytes 3072 | tf_op jit(solution)/shard_map/reshape | solution.py:711
  1.2 95.0 %guided_block.1 = bf16[1,384,384]{2,1,0:T(8,128)(2,1)} custom-call(s32[1,384]{1,0:T(1,128)} %reshape.6.clip_ref, s32[1,384]{1,0:T(1,128)} %bitcast.1, f32[3]{0:T(128)} %guide_ref.1, bf16[1,384,384]{2,1,0:T(8,128)(2,1)} %q_hbm.1, bf16[1,384,384]{2,1,0:T(8,128)(2,1)} %k_hbm.1, bf16[1,384,384]{2,1,0:T(8,128)(2,1)} %v_hbm.1, bf16[1,384,1536]{2,1,0:T(8,128)(2,1)} %res_hbm.1, ...), custom_call_target="tpu_custom_call" | custom-call | tf_op jit(solution)/shard_map/guided_block/pallas_call | solution.py:641
  96.3 1.7 %copy.13 = bf16[1,384,384]{2,1,0:T(8,128)(2,1)} copy(bf16[1,384,384]{2,1,0:T(8,128)(2,1)} %guided_block.1) | data formatting | bytes 589824

commit v4 on v3

--- a/solution.py
+++ b/solution.py
@@ -101,7 +101,7 @@
     transit,
     final,
     mine,
-    theirs,
+    base,
     placing,
     repack,
     going,
@@ -160,6 +160,7 @@
     barrier = pltpu.get_barrier_semaphore()
     peers = [along(t) for t in range(1, Z)] + [up(t) for t in range(1, Y)]
     peers += [over(t) for t in range(1, X)] + [other_core]
+    peers += [{**over(t), **other_core} for t in (1, 3)]
     for peer in peers:
         pl.semaphore_signal(barrier, inc=1, device_id=peer, device_id_type=MESH)
 
@@ -487,7 +488,8 @@
             centre = value - jnp.mean(value, axis=1, keepdims=True)
             spread = jnp.mean(centre * centre, axis=1, keepdims=True)
             scaled = centre * lax.rsqrt(spread + 1e-06) * (1.0 + mod[c, 2:3, :]) + mod[c, 1:2, :]
-            normed[rows, :] = scaled.astype(bf16)
+            to = pl.multiple_of((k // 2) * HALF + c * 64 + (k % 2) * 32, 32)
+            normed[pl.ds(to, 32), :] = scaled.astype(bf16)
         return carry
 
     lax.fori_loop(0, 4, normalise, 0)
@@ -513,29 +515,26 @@
     def chunk(k):
         return slice(128 * k, 128 * k + 128)
 
-    def give_far():
-        far_terms = contract(2).astype(bf16)
-        for k in range(3):
-            far[k] = far_terms[:, chunk(k)]
-            for way, rows in ((0, TOP), (1, LOW)):
-                passing[way, k] = remote(
-                    far.at[k, rows], transit.at[way, k],
-                    tsend.at[way, k], trecv.at[way, k], over((1, 3)[way]),
-                )
-                passing[way, k].start()
-
-    def give_near(way):
+    def give_far(k):
+        for way, rows in ((0, TOP), (1, LOW)):
+            passing[way, k] = remote(
+                far.at[k, rows], transit.at[way, k],
+                tsend.at[way, k], trecv.at[way, k], over((1, 3)[way]),
+            )
+            passing[way, k].start()
+
+    def near_terms(way):
         terms = contract((1, 3)[way])
         low = (HALF, 0)[way]
         for k in range(3):
             near[way, k] = terms[:, chunk(k)]
             ready[1 + way, k] = terms[low : low + HALF, chunk(k)].astype(bf16)
-            deliver(1 + way, k)
 
     def deliver(which, k):
         finals[which, k] = remote(
-            ready.at[which, k], final.at[which, k],
-            fsend.at[which, k], frecv.at[which, k], over((1, 1, 3, 3)[which]),
+            ready.at[which, k], final.at[side, which // 2, k],
+            fsend.at[which, k], frecv.at[side, which // 2, k],
+            {**over((1, 1, 3, 3)[which]), "cfg": which % 2},
         )
         finals[which, k].start()
 
@@ -545,40 +544,32 @@
             ready[which, k] = (near[way, k, rows, :] + transit[way, k].astype(f32)).astype(bf16)
             deliver(which, k)
 
-    exchanges, trips, last = {}, [], []
-
-    def finish(k):
-        for which in range(4):
-            finals[which, k].wait_recv()
+    trips, last = [], []
+    here = pl.ds(pl.multiple_of(z * 48, 16), 48)
+
+    def send_rows(k):
         cols = pl.ds(pl.multiple_of(blk * SLOTS + 128 * k, 128), 128)
+        for source in range(2):
+            for way in range(2):
+                remote(
+                    ready.at[way, k], final.at[source, way, k],
+                    fsend.at[way, k], frecv.at[source, way, k], over(1),
+                ).wait_recv()
+        guided = []
         for c in range(CLIPS):
-            for half in range(2):
-                start = c * 128 + half * 64
-                which, rows = start // HALF, slice(start % HALF, start % HALF + 64)
-                summed = own[start : start + 64, chunk(k)] + final[which, k, rows].astype(f32)
-                summed = summed + final[2 + which, k, rows].astype(f32)
-                value = mixed[start : start + 64, cols] + mod[c, 3:4, cols] * summed
-                mine[half, k, c * 64 : c * 64 + 64] = value.astype(bf16)
-        exchanges[k] = remote(
-            mine.at[1 - side, k], theirs.at[k], esend.at[k], erecv.at[k], other_core
-        )
-        exchanges[k].start()
-
-    here = pl.ds(pl.multiple_of(z * 48, 16), 48)
-
-    def send_rows(k):
-        exchanges[k].wait_recv()
-        ours, others = mine[side, k].astype(f32), theirs[k].astype(f32)
-        conditional = jnp.where(side == 0, ours, others)
-        plain = jnp.where(side == 0, others, ours)
-        guided = jnp.concatenate(
-            [
-                plain[64 * c : 64 * c + 64]
-                + guide_ref[c] * (conditional[64 * c : 64 * c + 64] - plain[64 * c : 64 * c + 64])
-                for c in range(CLIPS)
-            ],
-            axis=0,
-        ).astype(bf16)
+            rows = slice(64 * c, 64 * c + 64)
+            cond, uncond = (
+                (
+                    base[source, rows, chunk(k)]
+                    + mod[c, 3:4, cols]
+                    * (final[source, 0, k, rows].astype(f32) + final[source, 1, k, rows].astype(f32))
+                )
+                .astype(bf16)
+                .astype(f32)
+                for source in range(2)
+            )
+            guided.append((uncond + guide_ref[c] * (cond - uncond)).astype(bf16))
+        guided = jnp.concatenate(guided, axis=0)
         going[k] = jnp.dot(placing[...], guided, preferred_element_type=f32).astype(bf16)
         for t in NEAR_FIRST:
             there = pl.ds(pl.multiple_of(((z + t) % Z) * 48, 16), 48)
@@ -606,20 +597,40 @@
             last.append(copy)
         out_ref[0, row_here, 128 * k : 128 * k + 128] = turned[k, row_here, :]
 
-    give_far()
-    give_near(0)
-    give_near(1)
+    far_terms = contract(2).astype(bf16)
+    for k in range(3):
+        far[k] = far_terms[:, chunk(k)]
+    give_far(0)
+    give_far(1)
+    for way in range(2):
+        near_terms(way)
+        deliver(1 + way, 0)
+    own = contract(0)
+    own_cols = pl.ds(pl.multiple_of(blk * SLOTS, SLOTS), SLOTS)
+    for half in range(2):
+        for c in range(CLIPS):
+            at, start = c * 64, c * 128 + half * 64
+            mine[half, at : at + 64, :] = (
+                mixed[start : start + 64, own_cols]
+                + mod[c, 3:4, own_cols] * own[half * HALF + at : half * HALF + at + 64]
+            )
+    exchange = remote(mine.at[1 - side], base.at[side], esend.at[0], erecv.at[0], other_core)
+    exchange.start()
+    base[side] = mine[side]
+
     merge(0)
+    give_far(2)
+    deliver(1, 1)
+    deliver(2, 1)
     merge(1)
+    deliver(1, 2)
+    deliver(2, 2)
+    remote(mine.at[side], base.at[1 - side], esend.at[0], erecv.at[0], other_core).wait_recv()
+    send_rows(0)
     merge(2)
-    own = contract(0)
-    finish(0)
-    finish(1)
-    send_rows(0)
-    finish(2)
     send_rows(1)
+    send_rows(2)
     turn_rows(0)
-    send_rows(2)
     turn_rows(1)
     turn_rows(2)
     for copy in last:
@@ -629,7 +640,7 @@
         returning(t).wait_send()
     for copy in [
         *sends, *ring.values(), *gathers.values(), *passing.values(), *finals.values(),
-        *exchanges.values(), *trips,
+        exchange, *trips,
     ]:
         copy.wait_send()
 
@@ -676,9 +687,9 @@
             vmem((2, 3, SLOTS, 128), f32),
             vmem((4, 3, HALF, 128), bf16),
             vmem((2, 3, HALF, 128), bf16),
-            vmem((4, 3, HALF, 128), bf16),
-            vmem((2, 3, HALF, 128), bf16),
-            vmem((3, HALF, 128), bf16),
+            vmem((2, 2, 3, HALF, 128), bf16),
+            vmem((2, HALF, SLOTS), f32),
+            vmem((2, HALF, SLOTS), f32),
             vmem((SLOTS, HALF), bf16),
             vmem((SLOTS, SLOTS), bf16),
             vmem((3, SLOTS, 128), bf16),
@@ -692,8 +703,9 @@
             *[dma((4,))] * 4,
             *[dma((4, 2))] * 2,
             *[dma((2, 3))] * 2,
-            *[dma((4, 3))] * 2,
-            *[dma((3,))] * 2,
+            dma((4, 3)),
+            dma((2, 2, 3)),
+            *[dma((1,))] * 2,
             *[dma((3, Z))] * 2,
             *[dma((3, Y))] * 2,
         ],

time: 98.1 us -> 94.7 us (0.965)
  Pallas kernels: 95 us -> 90.7 us
    pallas_call x1, Pallas kernels: 95 us -> 90.7 us  [block(): pl.pallas_call(block_kernel, out_shape=jax.ShapeDtypeStruct((1, SLOTS, SL...]
where the time goes in v4:
time: 94.7 us; the launch traced here: 93.6 us
  Pallas kernels  90.7 us (96%)
  local copies, waits for them, and re-layouts  2.95 us (3%)
    pallas_call x1, Pallas kernels, block(): pl.pallas_call(block_kernel, out_shape=jax.ShapeDtypeStruct((1, SLOTS, SL...  90.7 us

profile of v4, /device:TPU:32, one launch (start us, length us, event | category | flops | bytes accessed | tf_op | source)
XLA Modules:
  0.0 93.6 jit_solution(13982528256698682906)
XLA Ops:
  0.0 1.2 %reshape.6.clip_ref = s32[1,384]{1,0:T(1,128)} reshape(s32[384]{0:T(512)} %param.20) | data formatting | bytes 3072 | tf_op jit(solution)/shard_map/reshape | solution.py:723
  1.2 90.7 %guided_block.1 = bf16[1,384,384]{2,1,0:T(8,128)(2,1)} custom-call(s32[1,384]{1,0:T(1,128)} %reshape.6.clip_ref, s32[1,384]{1,0:T(1,128)} %bitcast.1, f32[3]{0:T(128)} %guide_ref.1, bf16[1,384,384]{2,1,0:T(8,128)(2,1)} %q_hbm.1, bf16[1,384,384]{2,1,0:T(8,128)(2,1)} %k_hbm.1, bf16[1,384,384]{2,1,0:T(8,128)(2,1)} %v_hbm.1, bf16[1,384,1536]{2,1,0:T(8,128)(2,1)} %res_hbm.1, ...), custom_call_target="tpu_custom_call" | custom-call | tf_op jit(solution)/shard_map/guided_block/pallas_call | solution.py:652
  91.9 1.7 %copy.13 = bf16[1,384,384]{2,1,0:T(8,128)(2,1)} copy(bf16[1,384,384]{2,1,0:T(8,128)(2,1)} %guided_block.1) | data formatting | bytes 589824

commit v5 on v4

--- a/solution.py
+++ b/solution.py
@@ -179,10 +179,10 @@
             )
         )
     ]
-    for copy in loads:
+    for copy in loads[:3]:
         copy.start()
 
-    clips = clip_ref[...].astype(f32)
+    clips = clip_ref[...].reshape(1, SLOTS).astype(f32)
     first = clips[0:1, 0:1]
     count = jnp.sum(jnp.where(clips < CLIPS, 1.0, 0.0), axis=1, keepdims=True)
     row = lax.broadcasted_iota(jnp.int32, (SLOTS, SLOTS), 0).astype(f32)
@@ -248,6 +248,8 @@
         copy.start()
         shares.append(copy)
 
+    for copy in loads[3:]:
+        copy.start()
     kv9[0] = stage[8]
     q9[0] = stage[8, 0:128, :]
     best_s[...] = jnp.full_like(best_s, NEG_FILL)
@@ -261,7 +263,7 @@
         )
         ring[onto].start()
 
-    owners = owner_ref[...].astype(f32)
+    owners = owner_ref[...].reshape(1, SLOTS).astype(f32)
     owner_column = jnp.sum(jnp.where(row == lane, owners, 0.0), axis=1, keepdims=True)
     half_start = jnp.where(lane >= HALF, float(HALF), 0.0)
     earlier = (owner_column == owners) & (row < lane) & (row >= half_start)
@@ -331,7 +333,7 @@
             attend(j, tile)
             return carry
 
-        lax.fori_loop(0, 4, one, 0)
+        lax.fori_loop(0, 4, one, 0, unroll=True)
 
     for i, t in enumerate(NEAR_FIRST):
         sends[i].wait_recv()
@@ -341,9 +343,13 @@
             relay(7, 6, along(7))
     relay(2, 3, along(1))
     relay(6, 5, along(7))
+    for t in (0, 1, 7, 2):
+        for way in (0, 1):
+            from_row(way, t).wait_recv()
+        far_row(t).start()
     group(0)
     relay(3, 4, along(1))
-    for t in range(Z):
+    for t in (6, 3, 5, 4):
         for way in (0, 1):
             from_row(way, t).wait_recv()
         far_row(t).start()
@@ -371,7 +377,7 @@
                 stat_out[2 * tile + i, at : at + 8, :] = jnp.broadcast_to(line, (8, 128))
         return carry
 
-    lax.fori_loop(0, 2, ninth, 0)
+    lax.fori_loop(0, 2, ninth, 0, unroll=True)
     parts = []
     for j, onto, peer in ((1, 2, left), (2, 1, right), (3, 3, across)):
         for copy in (
@@ -396,7 +402,7 @@
         returning(2 * tile + 1).start()
         return carry
 
-    lax.fori_loop(0, 4, finish_tile, 0)
+    lax.fori_loop(0, 4, finish_tile, 0, unroll=True)
     own_block = pltpu.make_async_copy(out_stage.at[0], out_block(z), osend.at[0])
     own_block.start()
 
@@ -466,7 +472,7 @@
                 mixed[part, cols] += mod[c, 0:1, cols] * term[part]
             return carry
 
-        lax.fori_loop(0, 3, one, 0)
+        lax.fori_loop(0, 3, one, 0, unroll=True)
 
     gathers[1, 0].wait_recv()
     hop(1, 3, 0, over(1))
@@ -492,7 +498,7 @@
             normed[pl.ds(to, 32), :] = scaled.astype(bf16)
         return carry
 
-    lax.fori_loop(0, 4, normalise, 0)
+    lax.fori_loop(0, 4, normalise, 0, unroll=True)
 
     loads[6].wait()
 
@@ -502,7 +508,7 @@
         hidden[:, cols] = jax.nn.gelu(value, approximate=True).astype(bf16)
         return carry
 
-    lax.fori_loop(0, 3, expand, 0)
+    lax.fori_loop(0, 3, expand, 0, unroll=True)
 
     loads[7].wait()
 
@@ -571,7 +577,7 @@
             guided.append((uncond + guide_ref[c] * (cond - uncond)).astype(bf16))
         guided = jnp.concatenate(guided, axis=0)
         going[k] = jnp.dot(placing[...], guided, preferred_element_type=f32).astype(bf16)
-        for t in NEAR_FIRST:
+        for t in NEAR_FIRST[::-1]:
             there = pl.ds(pl.multiple_of(((z + t) % Z) * 48, 16), 48)
             copy = remote(
                 going.at[k, there], landed.at[k, here], gsend.at[k, t], grecv.at[k, t], along(t)
@@ -720,8 +726,8 @@
     queries, keys, values, residual, w_out, w_up, w_down, modulation, guide_scale, slot_clip, owner
 ):
     return block(
-        slot_clip.reshape(1, SLOTS),
-        owner.reshape(1, SLOTS),
+        slot_clip,
+        owner.reshape(SLOTS),
         guide_scale,
         queries,
         keys,

time: 94.7 us -> 91.7 us (0.968)
  Pallas kernels: 90.7 us -> 88.4 us
  other arithmetic: 0 us -> 1.27 us
  local copies, waits for them, and re-layouts: 2.95 us -> 1.71 us
    pallas_call x1, Pallas kernels: 90.7 us -> 88.4 us  [block(): pl.pallas_call(block_kernel, out_shape=jax.ShapeDtypeStruct((1, SLOTS, SL...]
    unnamed x0 -> x1, other arithmetic: none -> 1.27 us
    reshape x1 -> x0, local copies, waits for them, and re-layouts: 1.24 us -> none  [shards(): slot_clip.reshape(1, SLOTS)]
where the time goes in v5:
time: 91.7 us; the launch traced here: 91.4 us
  Pallas kernels  88.4 us (96%)
  local copies, waits for them, and re-layouts  1.71 us (2%)
  other arithmetic  1.27 us (1%)
    pallas_call x1, Pallas kernels, block(): pl.pallas_call(block_kernel, out_shape=jax.ShapeDtypeStruct((1, SLOTS, SL...  88.4 us

profile of v5, /device:TPU:32, one launch (start us, length us, event | category | flops | bytes accessed | tf_op | source)
XLA Modules:
  0.0 91.4 jit_solution(10197090966991699970)
XLA Ops:
  0.0 1.3 %reduce.owner_ref = s32[384]{0:T(512)} reduce(s32[384,1]{0,1:T(1,128)} %param.21, s32[]{:T(128)} %constant.4), dimensions={1}, to_apply=%param.21.reduce_sub_computation | reduce | bytes 3076 | tf_op args[10]
  1.3 88.4 %guided_block.1 = bf16[1,384,384]{2,1,0:T(8,128)(2,1)} custom-call(s32[384]{0:T(512)} %clip_ref.1, s32[384]{0:T(512)} %reduce.owner_ref, f32[3]{0:T(128)} %guide_ref.1, bf16[1,384,384]{2,1,0:T(8,128)(2,1)} %q_hbm.1, bf16[1,384,384]{2,1,0:T(8,128)(2,1)} %k_hbm.1, bf16[1,384,384]{2,1,0:T(8,128)(2,1)} %v_hbm.1, bf16[1,384,1536]{2,1,0:T(8,128)(2,1)} %res_hbm.1, ...), custom_call_target="tpu_custom_call" | custom-call | tf_op jit(solution)/shard_map/guided_block/pallas_call | solution.py:658
  89.7 1.7 %copy.13 = bf16[1,384,384]{2,1,0:T(8,128)(2,1)} copy(bf16[1,384,384]{2,1,0:T(8,128)(2,1)} %guided_block.1) | data formatting | bytes 589824

commit v6 on v5

--- a/solution.py
+++ b/solution.py
@@ -390,19 +390,14 @@
     for t in range(Z):
         far_row(t).wait()
 
-    def finish_tile(tile, carry):
+    for tile in (2, 1, 3, 0):
         total, accum = attend(3, tile)
         result = accum / jnp.sum(total, axis=1, keepdims=True)
         out_stage[pl.ds(2 * tile, 2)] = result.astype(bf16).reshape(2, 128, 128)
 
-        @pl.when(tile > 0)
-        def _():
+        if tile:
             returning(2 * tile).start()
-
         returning(2 * tile + 1).start()
-        return carry
-
-    lax.fori_loop(0, 4, finish_tile, 0, unroll=True)
     own_block = pltpu.make_async_copy(out_stage.at[0], out_block(z), osend.at[0])
     own_block.start()
 
@@ -611,6 +606,8 @@
     for way in range(2):
         near_terms(way)
         deliver(1 + way, 0)
+    merge(0)
+    give_far(2)
     own = contract(0)
     own_cols = pl.ds(pl.multiple_of(blk * SLOTS, SLOTS), SLOTS)
     for half in range(2):
@@ -624,8 +621,6 @@
     exchange.start()
     base[side] = mine[side]
 
-    merge(0)
-    give_far(2)
     deliver(1, 1)
     deliver(2, 1)
     merge(1)

time: 91.7 us -> 90.8 us (level)
  Pallas kernels: 88.4 us -> 87 us
    pallas_call x1, Pallas kernels: 88.4 us -> 87 us  [block(): pl.pallas_call(block_kernel, out_shape=jax.ShapeDtypeStruct((1, SLOTS, SL...]
where the time goes in v6:
time: 90.8 us; the launch traced here: 90 us
  Pallas kernels  87 us (96%)
  local copies, waits for them, and re-layouts  1.71 us (2%)
  other arithmetic  1.27 us (1%)
    pallas_call x1, Pallas kernels, block(): pl.pallas_call(block_kernel, out_shape=jax.ShapeDtypeStruct((1, SLOTS, SL...  87 us

profile of v6, /device:TPU:32, one launch (start us, length us, event | category | flops | bytes accessed | tf_op | source)
XLA Modules:
  0.0 90.0 jit_solution(14634671713490877886)
XLA Ops:
  0.0 1.3 %reduce.owner_ref = s32[384]{0:T(512)} reduce(s32[384,1]{0,1:T(1,128)} %param.21, s32[]{:T(128)} %constant.4), dimensions={1}, to_apply=%param.21.reduce_sub_computation | reduce | bytes 3076 | tf_op args[10]
  1.3 87.0 %guided_block.1 = bf16[1,384,384]{2,1,0:T(8,128)(2,1)} custom-call(s32[384]{0:T(512)} %clip_ref.1, s32[384]{0:T(512)} %reduce.owner_ref, f32[3]{0:T(128)} %guide_ref.1, bf16[1,384,384]{2,1,0:T(8,128)(2,1)} %q_hbm.1, bf16[1,384,384]{2,1,0:T(8,128)(2,1)} %k_hbm.1, bf16[1,384,384]{2,1,0:T(8,128)(2,1)} %v_hbm.1, bf16[1,384,1536]{2,1,0:T(8,128)(2,1)} %res_hbm.1, ...), custom_call_target="tpu_custom_call" | custom-call | tf_op jit(solution)/shard_map/guided_block/pallas_call | solution.py:653
  88.3 1.7 %copy.13 = bf16[1,384,384]{2,1,0:T(8,128)(2,1)} copy(bf16[1,384,384]{2,1,0:T(8,128)(2,1)} %guided_block.1) | data formatting | bytes 589824
